TPU v7x, 32 devices: a whole 2x2x4 slice. The times are simulated.
32 devices in a mesh: dp: 8 (over z, core), width: 4 (over y, x).
Axes of the slice: x: 2, y: 2, z: 4, core: 2. Of those that a mesh axis runs over, the one named last changes fastest.
Arguments:
- inputs: bfloat16 [1536, 4, 512], P('dp', 'width'), may hold values from -6 to 6
- block_weights: bfloat16 [4, 512, 3, 512], P('width'), may hold values from -0.15625 to 0.15625
- low_left: bfloat16 [4, 512, 256], P('width'), may hold values from -0.125 to 0.125
- low_right: bfloat16 [4, 256, 512], P('width'), may hold values from -0.375 to 0.375
- out_grad: bfloat16 [1536, 4, 512], P('dp', 'width'), may hold values from -6 to 6
Outputs:
- activations: bfloat16 [1536, 4, 512], P('dp', 'width')
- in_grad: bfloat16 [1536, 4, 512], P('dp', 'width')
- block_grad: float32 [4, 512, 3, 512], P('width', 'dp')
- left_grad: float32 [4, 512, 256], P('width', 'dp')
- right_grad: float32 [4, 256, 512], P('width', 'dp')
All inputs are finite; a program needn't handle non-finite values.
Results may differ from a plain program's by a relative error of at most 0.0061.
Values may be sent and summed in bfloat16 or wider, within the bound.
A program may use at most 64 MiB of HBM per device.

v0:
```python
import functools
import math

import jax
import jax.numpy as jnp
from jax import lax
from jax.experimental import pallas as pl
from jax.experimental.pallas import tpu as pltpu
from jax.sharding import PartitionSpec as P

root_half = 0.7071067811865476
inv_root_two_pi = 0.3989422804014327


def swapped(array, axis, apart):
    return lax.ppermute(array, axis, [(i, i ^ 1 << apart) for i in range(lax.axis_size(axis))])


def gelu_value(pre):
    return 0.5 * pre * (1.0 + lax.erf(pre * root_half))


def gelu_slope(pre):
    return (
        0.5 * (1.0 + lax.erf(pre * root_half)) + pre * jnp.exp(-0.5 * pre * pre) * inv_root_two_pi
    )


def plain_shards(inputs, block_weights, low_left, low_right, out_grad):
    own_x = inputs[:, 0]
    weights = block_weights[0]
    left = low_left[0]
    right = low_right[0]
    grad_out = out_grad[:, 0]
    levels = lax.axis_size("width").bit_length() - 1
    block_size = own_x.shape[1]
    scale = 1.0 / math.sqrt(own_x.shape[0] * lax.axis_size("dp"))
    pieces = [own_x]
    for bit in range(levels):
        pieces.append(swapped(own_x, "width", bit))
    all_x = jnp.stack(pieces, axis=1)
    latent = lax.psum(jnp.dot(own_x, left, preferred_element_type=jnp.float32), "width").astype(
        jnp.bfloat16
    )
    pre = lax.dot_general(
        all_x, weights, (((1, 2), (1, 2)), ((), ())), preferred_element_type=jnp.float32
    )
    pre = pre + jnp.dot(latent, right, preferred_element_type=jnp.float32)
    activations = gelu_value(pre).astype(jnp.bfloat16)
    hidden = (grad_out.astype(jnp.float32) * gelu_slope(pre)).astype(jnp.bfloat16)
    latent_term = lax.dot_general(
        hidden, right, (((1,), (1,)), ((), ())), preferred_element_type=jnp.float32
    )
    latent_grad = lax.psum(latent_term, "width").astype(jnp.bfloat16)
    partner_w = weights[:, 1:, :].reshape(weights.shape[0], levels * block_size)
    backs = jnp.dot(hidden, partner_w, preferred_element_type=jnp.float32).astype(jnp.bfloat16)
    returned = jnp.zeros(own_x.shape, jnp.float32)
    for bit in range(levels):
        piece = backs[:, bit * block_size : (bit + 1) * block_size]
        returned = returned + swapped(piece, "width", bit).astype(jnp.float32)
    own_back = jnp.dot(hidden, weights[:, 0, :], preferred_element_type=jnp.float32)
    own_back = own_back + lax.dot_general(
        latent_grad, left, (((1,), (1,)), ((), ())), preferred_element_type=jnp.float32
    )
    in_grad = (own_back + returned).astype(jnp.bfloat16)
    left_term = (
        lax.dot_general(
            own_x, latent_grad, (((0,), (0,)), ((), ())), preferred_element_type=jnp.float32
        )
        * scale
    )
    right_term = (
        lax.dot_general(
            latent, hidden, (((0,), (0,)), ((), ())), preferred_element_type=jnp.float32
        )
        * scale
    )
    block_term = (
        lax.dot_general(hidden, all_x, (((0,), (0,)), ((), ())), preferred_element_type=jnp.float32)
        * scale
    )
    block_grad, left_grad, right_grad = (
        lax.psum_scatter(block_term, "dp", scatter_dimension=0, tiled=True),
        lax.psum_scatter(left_term, "dp", scatter_dimension=0, tiled=True),
        lax.psum_scatter(right_term, "dp", scatter_dimension=0, tiled=True),
    )
    return (
        activations[:, None],
        in_grad[:, None],
        block_grad[None],
        left_grad[None],
        right_grad[None],
    )


f32 = jnp.float32
bf16 = jnp.bfloat16


def dot_nn(a, b):
    return jnp.dot(a, b, preferred_element_type=f32)


def dot_nt(a, b):
    return lax.dot_general(a, b, (((1,), (1,)), ((), ())), preferred_element_type=f32)


def remote(src, dst, send, recv, dp, width):
    return pltpu.make_async_remote_copy(
        src_ref=src,
        dst_ref=dst,
        send_sem=send,
        recv_sem=recv,
        device_id={"dp": dp, "width": width},
        device_id_type=pl.DeviceIdType.MESH,
    )


def step_kernel(
    n_dp, n_width, scale,
    x_hbm, w_hbm, left_hbm, right_hbm, g_hbm,
    act_out, in_out, block_out, left_out, right_out,
    x, w, left, right, g,
    xs, lat_sum, lat_own, lat_got, lat_full, lg_own, lg_got, hidden, x_t, h_t, lat_t,
    back_own, back_got, pre, own_back,
    main_away, main_own, main_core, main_send, main_lo, main_hi,
    low_away, low_own, low_core, low_send, low_lo, low_hi,
    load_sem, x_send, x_recv, lat_send, lat_recv, lg_send, lg_recv, back_send, back_recv,
    core_send, core_recv, line_send, lo_recv, hi_recv,
):
    levels = n_width.bit_length() - 1
    chips = n_dp // 2
    dp = lax.axis_index("dp")
    me = lax.axis_index("width")
    chip, core = dp // 2, dp % 2
    other_core = 1 - core
    twin = dp + 1 - 2 * core

    def mate(k):
        at = me
        for bit in range(levels):
            if k >> bit & 1:
                at = at + (1 << bit) * (1 - 2 * ((me // (1 << bit)) % 2))
        return at

    barrier = pltpu.get_barrier_semaphore()

    def greet(to_dp, to_width):
        pl.semaphore_signal(
            barrier,
            inc=1,
            device_id={"dp": to_dp, "width": to_width},
            device_id_type=pl.DeviceIdType.MESH,
        )

    for k in range(1, n_width):
        greet(dp, mate(k))
    greet(twin, me)

    @pl.when(chip > 0)
    def _():
        greet(dp - 2, me)

    @pl.when(chip < chips - 1)
    def _():
        greet(dp + 2, me)

    loads = [
        pltpu.make_async_copy(src, dst, load_sem.at[i])
        for i, (src, dst) in enumerate(
            ((x_hbm, x), (left_hbm, left), (w_hbm, w), (right_hbm, right), (g_hbm, g))
        )
    ]
    for load in loads:
        load.start()

    ends = jnp.where(chip == 0, 1, 0) + jnp.where(chip == chips - 1, 1, 0)
    pl.semaphore_wait(barrier, n_width + 2 - ends)

    loads[0].wait()
    tall = x.shape[0]
    share = tall // n_width
    halves = [slice(0, tall // 2), slice(tall // 2, tall)]
    x_copies = [
        [
            remote(
                x.at[half], xs.at[bit, half], x_send.at[part, bit], x_recv.at[part, bit],
                dp, mate(1 << bit),
            )
            for bit in range(levels)
        ]
        for part, half in enumerate(halves)
    ]

    def rows_of(device):
        return pl.ds(pl.multiple_of(device * share, share), share)

    loads[1].wait()
    lat_sum[...] = dot_nn(x[...], left[...])
    lat_own[...] = lat_sum[...].astype(bf16)
    lat_copies = [
        remote(
            lat_own.at[rows_of(mate(k))], lat_got.at[k - 1],
            lat_send.at[0, k - 1], lat_recv.at[0, k - 1], dp, mate(k),
        )
        for k in range(1, n_width)
    ]
    for copy in lat_copies + x_copies[0]:
        copy.start()
    loads[2].wait()
    pre[...] = dot_nt(x[...], w[0])
    for copy in lat_copies:
        copy.wait_recv()
    mine = lat_sum[rows_of(me), :]
    for k in range(n_width - 1):
        mine = mine + lat_got[k].astype(f32)
    lat_full[rows_of(me), :] = mine.astype(bf16)
    full_copies = [
        remote(
            lat_full.at[rows_of(me)], lat_full.at[rows_of(me)],
            lat_send.at[1, k - 1], lat_recv.at[1, k - 1], dp, mate(k),
        )
        for k in range(1, n_width)
    ]
    for copy in full_copies + x_copies[1]:
        copy.start()
    x_t[...] = x[...].astype(f32).T.astype(bf16).reshape(x_t.shape)
    loads[3].wait()
    loads[4].wait()
    for k in range(1, n_width):
        remote(
            lat_full.at[rows_of(mate(k))], lat_full.at[rows_of(mate(k))],
            lat_send.at[1, k - 1], lat_recv.at[1, k - 1], dp, mate(k),
        ).wait_recv()
    latent = lat_full[...]
    lat_t[...] = latent.astype(f32).T.astype(bf16).reshape(lat_t.shape)
    pre[...] += dot_nn(latent, right[...])
    for bit in range(levels):
        for part in range(2):
            x_copies[part][bit].wait_recv()
        pre[...] += dot_nt(xs[bit], w[bit + 1])

    v = pre[...]
    half = 0.5 * (1.0 + lax.erf(v * root_half))
    act_out[...] = (v * half).astype(bf16)
    slope = half + v * jnp.exp(-0.5 * v * v) * inv_root_two_pi
    hid = g[...].astype(f32) * slope
    hidden[...] = hid.astype(bf16)
    h = hidden[...]
    lg_mine = dot_nt(h, right[...])
    lg_own[...] = lg_mine.astype(bf16)
    lg_copies = [
        remote(lg_own, lg_got.at[k - 1], lg_send.at[k - 1], lg_recv.at[k - 1], dp, mate(k))
        for k in range(1, n_width)
    ]
    for copy in lg_copies:
        copy.start()
    h_t[...] = h.astype(f32).T.astype(bf16).reshape(h_t.shape)

    ob, rb = h_t.shape[2], lat_t.shape[2]
    rows = h_t.shape[3]

    last = levels + 1

    def main_terms(which, out_ref, level):
        lhs = h_t[:, which].reshape(chips * ob, rows)
        rhs = x[...] if level == 0 else xs[level - 1]
        term = dot_nn(lhs, rhs).astype(out_ref.dtype)
        out_ref[:, level * ob : (level + 1) * ob, :] = term.reshape(chips, ob, term.shape[1])
        if level == levels:
            lhs = lat_t[:, which].reshape(chips * rb, rows)
            term = dot_nn(lhs, hidden[...]).astype(out_ref.dtype)
            out_ref[:, last * ob :, :] = term.reshape(chips, rb, term.shape[1])

    far_first = []
    for k in range((chips + 1) // 2):
        far_first += [chips - 1 - k, k] if chips - 1 - k != k else [k]

    def part(main_ref, low_ref, s, c):
        if s == last:
            return low_ref.at[c]
        top = (s + 1) * ob + (rb if s == levels else 0)
        return main_ref.at[c, s * ob : top]

    def core_copy(s, c):
        return remote(
            part(main_away, low_away, s, c), part(main_core, low_core, s, c),
            core_send.at[s, c], core_recv.at[s, c], twin, me,
        )

    def up_copy(s, c, to):
        return remote(
            part(main_send, low_send, s, c), part(main_lo, low_lo, s, c),
            line_send.at[s, c], lo_recv.at[s, c], to, me,
        )

    def down_copy(s, c, to):
        return remote(
            part(main_send, low_send, s, c), part(main_hi, low_hi, s, c),
            line_send.at[s, c], hi_recv.at[s, c], to, me,
        )

    def pair_sum(s, c):
        core_copy(s, c).wait_recv()
        return part(main_own, low_own, s, c)[...] + part(main_core, low_core, s, c)[...].astype(f32)

    messages = [(k, s) for k in range(chips - 2) for s in range(last)]
    early = len(messages)
    messages += [(k, last) for k in range(chips - 2)]
    messages += [(chips - 2, s) for s in range(last + 1)]

    def hop(z, up, k, s):
        c = chips - 1 - k if up else k
        total = pair_sum(s, c)
        if up and z > 0:
            up_copy(s, c, dp + 2).wait_recv()
            total = total + part(main_lo, low_lo, s, c)[...].astype(f32)
        if not up and z < chips - 1:
            down_copy(s, c, dp - 2).wait_recv()
            total = total + part(main_hi, low_hi, s, c)[...].astype(f32)
        part(main_send, low_send, s, c)[...] = total.astype(bf16)
        if up:
            up_copy(s, c, dp + 2).start()
        else:
            down_copy(s, c, dp - 2).start()

    def hops(z):
        found = []
        for index, (k, s) in enumerate(messages):
            for up in (True, False):
                depth = z if up else chips - 1 - z
                if depth < chips - 1 and k < chips - 1 - depth:
                    found.append((2 * depth + index, depth, up, k, s))
        return [event[2:] for event in sorted(found)]

    for level in range(last):
        main_terms(other_core, main_away, level)
        for c in far_first:
            core_copy(level, c).start()
    for level in range(last):
        main_terms(core, main_own, level)
    back_copies = []
    for bit in range(levels):
        back_own[bit] = dot_nn(hidden[...], w[bit + 1]).astype(bf16)
        copy = remote(
            back_own.at[bit], back_got.at[bit], back_send.at[bit], back_recv.at[bit],
            dp, mate(1 << bit),
        )
        copy.start()
        back_copies.append(copy)

    for z in sorted({0, chips - 1}):

        @pl.when(chip == z)
        def _():
            for event in hops(z)[:early]:
                hop(z, *event)

    for copy in lg_copies:
        copy.wait_recv()
    for k in range(n_width - 1):
        lg_mine = lg_mine + lg_got[k].astype(f32)
    latent_grad = lg_mine.astype(bf16)

    def low_terms(which, out_ref):
        lhs = x_t[:, which].reshape(chips * x_t.shape[2], rows)
        term = dot_nn(lhs, latent_grad).astype(out_ref.dtype)
        out_ref[...] = term.reshape(out_ref.shape)

    low_terms(other_core, low_away)
    for c in far_first:
        core_copy(last, c).start()
    low_terms(core, low_own)
    own_back[...] = dot_nn(hidden[...], w[0]) + dot_nt(latent_grad, left[...])
    for z in range(chips):

        @pl.when(chip == z)
        def _():
            events = hops(z)
            for event in events[early:] if z in (0, chips - 1) else events:
                hop(z, *event)

    total = own_back[...]
    for bit in range(levels):
        back_copies[bit].wait_recv()
        total = total + back_got[bit].astype(f32)
    in_out[...] = total.astype(bf16)

    for z in range(chips):

        @pl.when(chip == z)
        def _():
            for s in range(last + 1):
                total = pair_sum(s, z)
                if z > 0:
                    up_copy(s, z, dp - 2).wait_recv()
                    total = total + part(main_lo, low_lo, s, z)[...].astype(f32)
                if z < chips - 1:
                    down_copy(s, z, dp + 2).wait_recv()
                    total = total + part(main_hi, low_hi, s, z)[...].astype(f32)
                if s == last:
                    left_out[...] = total * scale
                else:
                    block_out[s] = total[:ob] * scale
                if s == levels:
                    right_out[...] = total[ob:] * scale

    for copy in x_copies[0] + x_copies[1] + lat_copies + full_copies + lg_copies + back_copies:
        copy.wait_send()
    for s in range(last + 1):
        for c in range(chips):
            core_copy(s, c).wait_send()

            @pl.when(chip != c)
            def _():
                up_copy(s, c, twin).wait_send()


def hand_over(*refs):
    copies = [pltpu.make_async_copy(refs[i], refs[5 + i], refs[10].at[i]) for i in range(5)]
    for copy in copies:
        copy.start()
    for copy in copies:
        copy.wait()


def shards(inputs, block_weights, low_left, low_right, out_grad):
    n_dp, n_width = lax.axis_size("dp"), lax.axis_size("width")
    levels = n_width.bit_length() - 1
    rows, _, width_in = inputs.shape
    width_out = block_weights.shape[1]
    rank = low_left.shape[2]
    ob, ib, rb = width_out // n_dp, width_in // n_dp, rank // n_dp
    fits = n_dp % 2 == 0 and rows % (16 * n_width) == 0 and rows % 32 == 0 and width_in == width_out
    if not fits or ob % 16 or ib % 16 or rb % 16 or width_in % 128 or rank % 128:
        return plain_shards(inputs, block_weights, low_left, low_right, out_grad)
    chips = n_dp // 2
    scale = 1.0 / math.sqrt(rows * n_dp)
    main = (levels + 1) * ob + rb
    vm, dma = pltpu.VMEM, pltpu.SemaphoreType.DMA

    def line_scratch(r, c):
        return [
            vm((chips, r, c), bf16),
            vm((chips, r, c), f32),
            vm((chips, r, c), bf16),
            vm((chips, r, c), bf16),
            vm((chips, r, c), bf16),
            vm((chips, r, c), bf16),
        ]

    outs = pl.pallas_call(
        functools.partial(step_kernel, n_dp, n_width, scale),
        out_shape=(
            jax.ShapeDtypeStruct((rows, width_out), bf16),
            jax.ShapeDtypeStruct((rows, width_in), bf16),
            jax.ShapeDtypeStruct((levels + 1, ob, width_in), f32),
            jax.ShapeDtypeStruct((ib, rank), f32),
            jax.ShapeDtypeStruct((rb, width_out), f32),
        ),
        in_specs=[pl.BlockSpec(memory_space=pltpu.HBM)] * 5,
        out_specs=(pl.BlockSpec(memory_space=pltpu.VMEM),) * 5,
        scratch_shapes=[
            vm((rows, width_in), bf16),
            vm((levels + 1, width_out, width_in), bf16),
            vm((width_in, rank), bf16),
            vm((rank, width_out), bf16),
            vm((rows, width_out), bf16),
            vm((levels, rows, width_in), bf16),
            vm((rows, rank), f32),
            vm((rows, rank), bf16),
            vm((n_width - 1, rows // n_width, rank), bf16),
            vm((rows, rank), bf16),
            vm((rows, rank), bf16),
            vm((n_width - 1, rows, rank), bf16),
            vm((rows, width_out), bf16),
            vm((chips, 2, ib, rows), bf16),
            vm((chips, 2, ob, rows), bf16),
            vm((chips, 2, rb, rows), bf16),
            vm((levels, rows, width_in), bf16),
            vm((levels, rows, width_in), bf16),
            vm((rows, width_out), f32),
            vm((rows, width_in), f32),
            *line_scratch(main, width_in),
            *line_scratch(ib, rank),
            dma((5,)),
            dma((2, levels)),
            dma((2, levels)),
            dma((2, n_width - 1)),
            dma((2, n_width - 1)),
            dma((n_width - 1,)),
            dma((n_width - 1,)),
            dma((levels,)),
            dma((levels,)),
            dma((levels + 2, chips)),
            dma((levels + 2, chips)),
            dma((levels + 2, chips)),
            dma((levels + 2, chips)),
            dma((levels + 2, chips)),
        ],
        compiler_params=pltpu.CompilerParams(
            collective_id=0, has_side_effects=True, vmem_limit_bytes=40 * 1024 * 1024
        ),
    )(
        *(
            pltpu.with_memory_space_constraint(array, pltpu.HBM)
            for array in (
                inputs[:, 0],
                block_weights[0].transpose(1, 0, 2),
                low_left[0],
                low_right[0],
                out_grad[:, 0],
            )
        )
    )
    act, in_grad, block, left, right = pl.pallas_call(
        hand_over,
        out_shape=tuple(jax.ShapeDtypeStruct(out.shape, out.dtype) for out in outs),
        in_specs=[pl.BlockSpec(memory_space=pltpu.VMEM)] * 5,
        out_specs=(pl.BlockSpec(memory_space=pl.ANY),) * 5,
        scratch_shapes=[dma((5,))],
        compiler_params=pltpu.CompilerParams(vmem_limit_bytes=4 * 1024 * 1024),
    )(*outs)
    return (
        act[:, None],
        in_grad[:, None],
        block.transpose(1, 0, 2)[None],
        left[None],
        right[None],
    )


def solution(mesh):
    placed = (
        P("dp", "width", None),
        P("width", None, None, None),
        P("width", None, None),
        P("width", None, None),
        P("dp", "width", None),
    )
    return jax.shard_map(
        shards,
        mesh=mesh,
        in_specs=placed,
        out_specs=(
            P("dp", "width", None),
            P("dp", "width", None),
            P("width", "dp", None, None),
            P("width", "dp", None),
            P("width", "dp", None),
        ),
        check_vma=False,
    )
```

profile of v0, /device:TPU:0, one launch (start us, length us, event | category | flops | bytes accessed | tf_op | source)
XLA Modules:
  0.0 38.8 jit_solution(10618928645749682664)
XLA Ops:
  0.6 37.2 %shard_map.92 = (bf16[192,512]{1,0:T(8,128)(2,1)S(1)}, bf16[192,512]{1,0:T(8,128)(2,1)S(1)}, f32[3,64,512]{2,1,0:T(8,128)S(1)}, f32[64,256]{1,0:T(8,128)S(1)}, f32[32,512]{1,0:T(8,128)S(1)}) custom-call(bf16[192,512]{1,0:T(8,128)(2,1)} %bitcast.17, bf16[3,512,512]{2,1,0:T(8,128)(2,1)} %bitcast.14, bf16[512,256]{1,0:T(8,128)(2,1)} %bitcast.15, ...), custom_call_target="tpu_custom_call" | custom-call | tf_op jit(solution)/shard_map/pallas_call | solution.py:452
  37.9 1.0 %shard_map.93 = (bf16[192,512]{1,0:T(8,128)(2,1)}, bf16[192,512]{1,0:T(8,128)(2,1)}, f32[3,64,512]{2,1,0:T(8,128)}, f32[64,256]{1,0:T(8,128)}, f32[32,512]{1,0:T(8,128)}) custom-call(bf16[192,512]{1,0:T(8,128)(2,1)S(1)} %get-tuple-element.15.refs_0_, bf16[192,512]{1,0:T(8,128)(2,1)S(1)} %get-tuple-element.16.refs_1_, ...), custom_call_target="tpu_custom_call" | custom-call | tf_op jit(solution)/shard_map/pallas_call | solution.py:516
where the time goes:
time: 39 us; the launch traced here: 38.8 us
  Pallas kernels  38.2 us (98%)
  between operations  0.64 us (2%)
    pallas_call x1, Pallas kernels, shards(): pl.pallas_call(functools.partial(step_kernel, n_dp, n_width, scale), out_...  37.2 us
    pallas_call x1, Pallas kernels, shards(): pl.pallas_call(hand_over, out_shape=tuple((jax.ShapeDtypeStruct(out.shape...  0.96 us

commit v1 on v0

v1 whole, which is shorter than its diff:
```python
import functools
import math

import jax
import jax.numpy as jnp
from jax import lax
from jax.experimental import pallas as pl
from jax.experimental.pallas import tpu as pltpu
from jax.sharding import PartitionSpec as P

root_half = 0.7071067811865476
inv_root_two_pi = 0.3989422804014327
chips_in_line = 4


def swapped(array, axis, apart):
    return lax.ppermute(array, axis, [(i, i ^ 1 << apart) for i in range(lax.axis_size(axis))])


def gelu_value(pre):
    return 0.5 * pre * (1.0 + lax.erf(pre * root_half))


def gelu_slope(pre):
    return (
        0.5 * (1.0 + lax.erf(pre * root_half)) + pre * jnp.exp(-0.5 * pre * pre) * inv_root_two_pi
    )


def plain_shards(inputs, block_weights, low_left, low_right, out_grad):
    own_x = inputs[:, 0]
    weights = block_weights[0]
    left = low_left[0]
    right = low_right[0]
    grad_out = out_grad[:, 0]
    levels = lax.axis_size("width").bit_length() - 1
    block_size = own_x.shape[1]
    scale = 1.0 / math.sqrt(own_x.shape[0] * lax.axis_size("dp"))
    pieces = [own_x]
    for bit in range(levels):
        pieces.append(swapped(own_x, "width", bit))
    all_x = jnp.stack(pieces, axis=1)
    latent = lax.psum(jnp.dot(own_x, left, preferred_element_type=jnp.float32), "width").astype(
        jnp.bfloat16
    )
    pre = lax.dot_general(
        all_x, weights, (((1, 2), (1, 2)), ((), ())), preferred_element_type=jnp.float32
    )
    pre = pre + jnp.dot(latent, right, preferred_element_type=jnp.float32)
    activations = gelu_value(pre).astype(jnp.bfloat16)
    hidden = (grad_out.astype(jnp.float32) * gelu_slope(pre)).astype(jnp.bfloat16)
    latent_term = lax.dot_general(
        hidden, right, (((1,), (1,)), ((), ())), preferred_element_type=jnp.float32
    )
    latent_grad = lax.psum(latent_term, "width").astype(jnp.bfloat16)
    partner_w = weights[:, 1:, :].reshape(weights.shape[0], levels * block_size)
    backs = jnp.dot(hidden, partner_w, preferred_element_type=jnp.float32).astype(jnp.bfloat16)
    returned = jnp.zeros(own_x.shape, jnp.float32)
    for bit in range(levels):
        piece = backs[:, bit * block_size : (bit + 1) * block_size]
        returned = returned + swapped(piece, "width", bit).astype(jnp.float32)
    own_back = jnp.dot(hidden, weights[:, 0, :], preferred_element_type=jnp.float32)
    own_back = own_back + lax.dot_general(
        latent_grad, left, (((1,), (1,)), ((), ())), preferred_element_type=jnp.float32
    )
    in_grad = (own_back + returned).astype(jnp.bfloat16)
    left_term = (
        lax.dot_general(
            own_x, latent_grad, (((0,), (0,)), ((), ())), preferred_element_type=jnp.float32
        )
        * scale
    )
    right_term = (
        lax.dot_general(
            latent, hidden, (((0,), (0,)), ((), ())), preferred_element_type=jnp.float32
        )
        * scale
    )
    block_term = (
        lax.dot_general(hidden, all_x, (((0,), (0,)), ((), ())), preferred_element_type=jnp.float32)
        * scale
    )
    block_grad, left_grad, right_grad = (
        lax.psum_scatter(block_term, "dp", scatter_dimension=0, tiled=True),
        lax.psum_scatter(left_term, "dp", scatter_dimension=0, tiled=True),
        lax.psum_scatter(right_term, "dp", scatter_dimension=0, tiled=True),
    )
    return (
        activations[:, None],
        in_grad[:, None],
        block_grad[None],
        left_grad[None],
        right_grad[None],
    )


f32 = jnp.float32
bf16 = jnp.bfloat16


def dot_nn(a, b):
    return jnp.dot(a, b, preferred_element_type=f32)


def dot_nt(a, b):
    return lax.dot_general(a, b, (((1,), (1,)), ((), ())), preferred_element_type=f32)


def remote(src, dst, send, recv, dp, width):
    return pltpu.make_async_remote_copy(
        src_ref=src,
        dst_ref=dst,
        send_sem=send,
        recv_sem=recv,
        device_id={"dp": dp, "width": width},
        device_id_type=pl.DeviceIdType.MESH,
    )


def step_kernel(
    n_dp, n_width, scale,
    x_hbm, w_hbm, left_hbm, right_hbm, g_hbm,
    act_out, in_out, block_out, left_out, right_out,
    x, w, left, right, g,
    lat_sum, lat_own, lat_got, lat, lg_own, lg_got, lg, hidden,
    x_t, x_u, h_t, h_u, lat_t, lat_u, far_acc,
    back_own, back_got, pre,
    away_b, own_b, core_b, far_b, near_b, end_b, fin_b,
    away_r, own_r, core_r, far_r, near_r, end_r, fin_r,
    away_l, own_l, core_l, far_l, near_l, end_l, fin_l,
    load_sem, x_send, x_recv, lat_send, lat_recv, lg_send, lg_recv, back_send, back_recv,
    up_send, up_recv, side_send, side_recv,
    core_send, core_recv, mid_send, mid_recv, end_send, end_recv,
):
    levels = n_width.bit_length() - 1
    chips = n_dp // 2
    dp = lax.axis_index("dp")
    me = lax.axis_index("width")
    chip, core = dp // 2, dp % 2
    other_core = 1 - core
    twin = dp + 1 - 2 * core
    side = chip // 2
    outer = (chip + side) % 2
    is_end = outer == 0
    is_hub = outer == 1
    step = 2 - 4 * side
    hub_dp = dp + step
    end_dp = dp - step
    far_dp = dp + step

    def mate(k):
        at = me
        for bit in range(levels):
            if k >> bit & 1:
                at = at + (1 << bit) * (1 - 2 * ((me // (1 << bit)) % 2))
        return at

    def shard(p):
        first = (3, 2, 0, 1)[p]
        return first + side * (chips - 1 - 2 * first)

    barrier = pltpu.get_barrier_semaphore()

    def greet(to_dp, to_width):
        pl.semaphore_signal(
            barrier,
            inc=1,
            device_id={"dp": to_dp, "width": to_width},
            device_id_type=pl.DeviceIdType.MESH,
        )

    for k in range(1, n_width):
        greet(dp, mate(k))
    greet(twin, me)

    @pl.when(chip > 0)
    def _():
        greet(dp - 2, me)

    @pl.when(chip < chips - 1)
    def _():
        greet(dp + 2, me)

    rows = x_hbm.shape[0]
    mine, theirs = pl.ds(0, rows), pl.ds(rows, rows)
    loads = [
        pltpu.make_async_copy(src, dst, load_sem.at[i])
        for i, (src, dst) in enumerate(
            (
                (x_hbm, x.at[0, mine]),
                (left_hbm, left),
                (w_hbm, w),
                (right_hbm, right),
                (g_hbm, g),
            )
        )
    ]
    for load in loads:
        load.start()

    ends = jnp.where(chip == 0, 1, 0) + jnp.where(chip == chips - 1, 1, 0)
    pl.semaphore_wait(barrier, n_width + 2 - ends)

    loads[0].wait()
    cut = rows // levels
    parts = [pl.ds(j * cut, cut) for j in range(levels)]
    beyond = [pl.ds(rows + j * cut, cut) for j in range(levels)]
    x_copies = [
        [
            remote(
                x.at[0, part], x.at[bit + 1, part], x_send.at[j, bit], x_recv.at[j, bit],
                dp, mate(1 << bit),
            )
            for bit in range(levels)
        ]
        for j, part in enumerate(parts)
    ]

    def exchange(sums, out, got, send, recv, t):
        copies = []
        for j, part in enumerate(parts):
            out[t, part] = sums[part].astype(bf16)
            copies.append(
                remote(
                    out.at[t, part], got.at[t, part], send.at[t, j], recv.at[t, j],
                    dp, mate(1 << (j + t) % levels),
                )
            )
        for copy in copies:
            copy.start()
        return copies

    def merge(copies, sums, got, t, j):
        copies[j].wait_recv()
        sums[parts[j]] += got[t, parts[j]].astype(f32)

    up_x = remote(x.at[0, mine], x.at[0, theirs], up_send.at[0], up_recv.at[0], hub_dp, me)
    side_copies = [
        remote(
            x.at[0, theirs], x.at[bit + 1, theirs], side_send.at[bit], side_recv.at[bit],
            dp, mate(1 << bit),
        )
        for bit in range(levels)
    ]

    @pl.when(is_end)
    def _():
        up_x.start()

    loads[1].wait()
    lat_sum[...] = dot_nn(x[0, mine], left[...])
    lat_copies = [exchange(lat_sum, lat_own, lat_got, lat_send, lat_recv, 0)]
    for copy in x_copies[0]:
        copy.start()
    loads[2].wait()
    pre[...] = dot_nt(x[0, mine], w[0])
    for t in range(1, levels):
        for j in range(levels):
            merge(lat_copies[-1], lat_sum, lat_got, t - 1, j)
        lat_copies.append(exchange(lat_sum, lat_own, lat_got, lat_send, lat_recv, t))
        for copy in x_copies[t]:
            copy.start()
    loads[3].wait()
    loads[4].wait()

    ob, rb, ib = h_t.shape[2], lat_t.shape[2], x_t.shape[2]
    last = levels + 1

    def span(p, size):
        return pl.ds(pl.multiple_of(shard(p) * size, size), size)

    up_h = [
        [
            remote(
                hidden.at[part, span(p, 2 * ob)], hidden.at[away_part, span(p, 2 * ob)],
                up_send.at[2 + levels + chips * j + p], up_recv.at[2 + levels + chips * j + p],
                hub_dp, me,
            )
            for p in range(chips)
        ]
        for j, (part, away_part) in enumerate(zip(parts, beyond))
    ]
    up_lat = [
        remote(
            lat.at[part], lat.at[away_part], up_send.at[2 + j], up_recv.at[2 + j], hub_dp, me
        )
        for j, (part, away_part) in enumerate(zip(parts, beyond))
    ]
    up_lg = remote(lg.at[mine], lg.at[theirs], up_send.at[1], up_recv.at[1], hub_dp, me)

    for j, part in enumerate(parts):
        merge(lat_copies[-1], lat_sum, lat_got, levels - 1, j)
        lat[part, :] = lat_sum[part, :].astype(bf16)
        v = pre[part, :] + dot_nn(lat[part, :], right[...])
        for bit in range(levels):
            x_copies[j][bit].wait_recv()
            v = v + dot_nt(x[bit + 1, part], w[bit + 1])
        half = 0.5 * (1.0 + lax.erf(v * root_half))
        act_out[part, :] = (v * half).astype(bf16)
        slope = half + v * jnp.exp(-0.5 * v * v) * inv_root_two_pi
        hidden[part, :] = (g[part, :].astype(f32) * slope).astype(bf16)

        @pl.when(is_end)
        def _():
            for p in range(2):
                up_h[j][p].start()
            up_lat[j].start()

        if j == 0:

            @pl.when(is_hub)
            def _():
                up_x.wait_recv()
                for copy in side_copies:
                    copy.start()


    lat_sum[...] = dot_nt(hidden[mine, :], right[...])
    lg_copies = [exchange(lat_sum, lg_own, lg_got, lg_send, lg_recv, 0)]

    def pick(kind, s):
        block, low_right, low_left = kind
        if s < last:
            return block.at[s]
        return low_right if s == last else low_left

    away = (away_b, away_r, away_l)
    own = (own_b, own_r, own_l)
    cored = (core_b, core_r, core_l)
    far = (far_b, far_r, far_l)
    near = (near_b, near_r, near_l)
    ended = (end_b, end_r, end_l)
    fin = (fin_b, fin_r, fin_l)
    segments = range(last + 2)

    def core_copy(s, p):
        return remote(
            pick(away, s).at[p], pick(cored, s).at[p], core_send.at[s, p], core_recv.at[s, p],
            twin, me,
        )

    def mid_copy(s, p):
        return remote(
            pick(far, s).at[p], pick(near, s).at[p], mid_send.at[s, p], mid_recv.at[s, p],
            far_dp, me,
        )

    def end_copy(s):
        return remote(
            pick(ended, s), pick(fin, s), end_send.at[s], end_recv.at[s], end_dp, me
        )

    def put(s, total):
        if s < last:
            block_out[s] = total * scale
        elif s == last:
            right_out[...] = total * scale
        else:
            left_out[...] = total * scale

    back_copies = [
        remote(
            back_own.at[bit], back_got.at[bit], back_send.at[bit], back_recv.at[bit],
            dp, mate(1 << bit),
        )
        for bit in range(levels)
    ]

    def lg_step(t):
        for j in range(levels):
            merge(lg_copies[-1], lat_sum, lg_got, t - 1, j)
        if t < levels:
            lg_copies.append(exchange(lat_sum, lg_own, lg_got, lg_send, lg_recv, t))
        else:
            lg[mine, :] = lat_sum[...].astype(bf16)

    def send_back():
        for bit in range(levels):
            back_own[bit] = dot_nn(hidden[mine, :], w[bit + 1]).astype(bf16)
            back_copies[bit].start()

    def back_ready():
        total = dot_nn(hidden[mine, :], w[0]) + dot_nt(lg[mine, :], left[...])
        for bit in range(levels):
            back_copies[bit].wait_recv()
            total = total + back_got[bit].astype(f32)
        in_out[...] = total.astype(bf16)

    def sent():
        for group in x_copies + lat_copies + lg_copies + [back_copies]:
            for copy in group:
                copy.wait_send()

    @pl.when(is_end)
    def _():
        for j in range(levels):
            for p in range(2, chips):
                up_h[j][p].start()
        for t in range(1, levels + 1):
            lg_step(t)
            if t == levels - 1:
                send_back()
        up_lg.start()
        back_ready()
        sent()
        up_x.wait_send()
        up_lg.wait_send()
        for j in range(levels):
            up_lat[j].wait_send()
            for p in range(chips):
                up_h[j][p].wait_send()
        for s in segments:
            end_copy(s).wait_recv()
            put(s, pick(fin, s)[...].astype(f32))

    del lg_copies[1:]

    @pl.when(is_hub)
    def _():
        def turn(ref, which, p, size):
            tall = ref[which, span(p, size)].astype(f32).T.astype(bf16)
            return tall.reshape(2, size // 2, rows)

        def stack(ref, which, positions):
            return jnp.concatenate([ref[p, which] for p in positions], axis=0)

        def own_rows(s, which, positions):
            if s < last:
                return dot_nn(stack(h_t, which, positions), x[s, mine])
            if s == last:
                return dot_nn(stack(lat_t, which, [shard(p) for p in positions]), hidden[mine, :])
            return dot_nn(stack(x_t, which, positions), lg[mine, :])

        def their_rows(s, which, positions):
            if s < last:
                return dot_nn(stack(h_u, which, positions), x[s, theirs])
            if s == last:
                return dot_nn(stack(lat_u, which, [shard(p) for p in positions]), hidden[theirs, :])
            return dot_nn(stack(x_u, which, positions), lg[theirs, :])

        def put_terms(s, positions, to_other, to_own):
            shape = pick(own, s).shape[1:]
            for i, p in enumerate(positions):
                these = slice(i * shape[0], (i + 1) * shape[0])
                pick(away, s)[p] = to_other[these].astype(bf16)
                core_copy(s, p).start()
            for i, p in enumerate(positions):
                these = slice(i * shape[0], (i + 1) * shape[0])
                pick(own, s)[p] = to_own[these]

        def terms(s, positions):
            first = own_rows(s, other_core, positions) + their_rows(s, other_core, positions)
            put_terms(
                s, positions, first, own_rows(s, core, positions) + their_rows(s, core, positions)
            )

        def far_terms(s, positions):
            size = len(positions) * ob
            held = slice(positions[0], positions[0] + len(positions))
            first = far_acc[s, held].reshape(size, far_acc.shape[3])
            second = own_b[s, held].reshape(size, far_acc.shape[3])
            put_terms(
                s, positions, first + their_rows(s, other_core, positions),
                second + their_rows(s, core, positions),
            )

        def pair(s, p):
            return pick(own, s)[p] + pick(cored, s)[p].astype(f32)

        def send_far(s, p):
            core_copy(s, p).wait_recv()
            pick(far, s)[p] = pair(s, p).astype(bf16)
            mid_copy(s, p).start()

        for p in range(2):
            h_t[p] = turn(hidden, mine, p, 2 * ob)
        for s in range(last):
            shape = (2, ob, far_acc.shape[3])
            far_acc[s] = own_rows(s, other_core, range(2)).reshape(shape)
            own_b[s, 0:2] = own_rows(s, core, range(2)).reshape(shape)
        for p in range(2):
            for j in range(levels):
                up_h[j][p].wait_recv()
            h_u[p] = turn(hidden, theirs, p, 2 * ob)
            far_terms(0, [p])
        for p in range(2):
            send_far(0, p)
        for bit in range(levels):
            side_copies[bit].wait_recv()
            far_terms(bit + 1, [0, 1])
        for t in range(1, levels):
            lg_step(t)
        send_back()
        for s in range(1, last):
            for p in range(2):
                send_far(s, p)
        for j in range(levels):
            up_lat[j].wait_recv()
        lat_t[...] = lat[mine, :].astype(f32).T.astype(bf16).reshape(lat_t.shape)
        lat_u[...] = lat[theirs, :].astype(f32).T.astype(bf16).reshape(lat_t.shape)
        for p in range(2, chips):
            for j in range(levels):
                up_h[j][p].wait_recv()
        terms(last, range(2))
        for p in range(2, chips):
            h_t[p] = turn(hidden, mine, p, 2 * ob)
            h_u[p] = turn(hidden, theirs, p, 2 * ob)
        for s in range(last):
            terms(s, range(2, chips))
        terms(last, range(2, chips))
        for p in range(chips):
            x_t[p] = turn(x.at[0], mine, p, 2 * ib)
            x_u[p] = turn(x.at[0], theirs, p, 2 * ib)
        lg_step(levels)
        up_lg.wait_recv()
        terms(last + 1, range(2))
        for p in range(2):
            send_far(last, p)
            send_far(last + 1, p)
        terms(last + 1, range(2, chips))

        def send_end(s):
            core_copy(s, 2).wait_recv()
            mid_copy(s, 0).wait_recv()
            pick(ended, s)[...] = (pair(s, 2) + pick(near, s)[0].astype(f32)).astype(bf16)
            end_copy(s).start()

        def keep(s):
            core_copy(s, 3).wait_recv()
            mid_copy(s, 1).wait_recv()
            put(s, pair(s, 3) + pick(near, s)[1].astype(f32))

        for s in range(last):
            send_end(s)
            keep(s)
        back_ready()
        sent()
        for copy in side_copies:
            copy.wait_send()
        for s in segments:
            for p in range(chips):
                core_copy(s, p).wait_send()
        send_end(last)
        send_end(last + 1)
        keep(last)
        keep(last + 1)
        for s in segments:
            for p in range(2):
                mid_copy(s, p).wait_send()
            end_copy(s).wait_send()


def hand_over(*refs):
    copies = [pltpu.make_async_copy(refs[i], refs[5 + i], refs[10].at[i]) for i in range(5)]
    for copy in copies:
        copy.start()
    for copy in copies:
        copy.wait()


def shards(inputs, block_weights, low_left, low_right, out_grad):
    n_dp, n_width = lax.axis_size("dp"), lax.axis_size("width")
    levels = n_width.bit_length() - 1
    rows, _, width_in = inputs.shape
    width_out = block_weights.shape[1]
    rank = low_left.shape[2]
    ob, ib, rb = width_out // n_dp, width_in // n_dp, rank // n_dp
    fits = n_dp == 2 * chips_in_line and rows % (16 * n_width) == 0 and rows % 32 == 0 and width_in == width_out
    if not fits or ob % 64 or ib % 64 or rb % 16 or levels < 1 or rows % (16 * levels) or rank % 128:
        return plain_shards(inputs, block_weights, low_left, low_right, out_grad)
    chips = n_dp // 2
    scale = 1.0 / math.sqrt(rows * n_dp)
    vm, dma = pltpu.VMEM, pltpu.SemaphoreType.DMA

    def line_scratch(lead, r, c):
        return [
            vm((*lead, chips, r, c), bf16),
            vm((*lead, chips, r, c), f32),
            vm((*lead, chips, r, c), bf16),
            vm((*lead, 2, r, c), bf16),
            vm((*lead, 2, r, c), bf16),
            vm((*lead, r, c), bf16),
            vm((*lead, r, c), bf16),
        ]

    outs = pl.pallas_call(
        functools.partial(step_kernel, n_dp, n_width, scale),
        out_shape=(
            jax.ShapeDtypeStruct((rows, width_out), bf16),
            jax.ShapeDtypeStruct((rows, width_in), bf16),
            jax.ShapeDtypeStruct((levels + 1, ob, width_in), f32),
            jax.ShapeDtypeStruct((ib, rank), f32),
            jax.ShapeDtypeStruct((rb, width_out), f32),
        ),
        in_specs=[pl.BlockSpec(memory_space=pltpu.HBM)] * 5,
        out_specs=(pl.BlockSpec(memory_space=pltpu.VMEM),) * 5,
        scratch_shapes=[
            vm((levels + 1, 2 * rows, width_in), bf16),
            vm((levels + 1, width_out, width_in), bf16),
            vm((width_in, rank), bf16),
            vm((rank, width_out), bf16),
            vm((rows, width_out), bf16),
            vm((rows, rank), f32),
            vm((levels, rows, rank), bf16),
            vm((levels, rows, rank), bf16),
            vm((2 * rows, rank), bf16),
            vm((levels, rows, rank), bf16),
            vm((levels, rows, rank), bf16),
            vm((2 * rows, rank), bf16),
            vm((2 * rows, width_out), bf16),
            vm((chips, 2, ib, rows), bf16),
            vm((chips, 2, ib, rows), bf16),
            vm((chips, 2, ob, rows), bf16),
            vm((chips, 2, ob, rows), bf16),
            vm((chips, 2, rb, rows), bf16),
            vm((chips, 2, rb, rows), bf16),
            vm((levels + 1, 2, ob, width_in), f32),
            vm((levels, rows, width_in), bf16),
            vm((levels, rows, width_in), bf16),
            vm((rows, width_out), f32),
            *line_scratch((levels + 1,), ob, width_in),
            *line_scratch((), rb, width_out),
            *line_scratch((), ib, rank),
            dma((5,)),
            dma((levels, levels)),
            dma((levels, levels)),
            dma((levels, levels)),
            dma((levels, levels)),
            dma((levels, levels)),
            dma((levels, levels)),
            dma((levels,)),
            dma((levels,)),
            dma((2 + levels * (1 + chips),)),
            dma((2 + levels * (1 + chips),)),
            dma((levels,)),
            dma((levels,)),
            dma((levels + 3, chips)),
            dma((levels + 3, chips)),
            dma((levels + 3, 2)),
            dma((levels + 3, 2)),
            dma((levels + 3,)),
            dma((levels + 3,)),
        ],
        compiler_params=pltpu.CompilerParams(
            collective_id=0, has_side_effects=True, vmem_limit_bytes=40 * 1024 * 1024
        ),
    )(
        *(
            pltpu.with_memory_space_constraint(array, pltpu.HBM)
            for array in (
                inputs[:, 0],
                block_weights[0].transpose(1, 0, 2),
                low_left[0],
                low_right[0],
                out_grad[:, 0],
            )
        )
    )
    act, in_grad, block, left, right = pl.pallas_call(
        hand_over,
        out_shape=tuple(jax.ShapeDtypeStruct(out.shape, out.dtype) for out in outs),
        in_specs=[pl.BlockSpec(memory_space=pltpu.VMEM)] * 5,
        out_specs=(pl.BlockSpec(memory_space=pl.ANY),) * 5,
        scratch_shapes=[dma((5,))],
        compiler_params=pltpu.CompilerParams(vmem_limit_bytes=4 * 1024 * 1024),
    )(*outs)
    return (
        act[:, None],
        in_grad[:, None],
        block.transpose(1, 0, 2)[None],
        left[None],
        right[None],
    )


def solution(mesh):
    placed = (
        P("dp", "width", None),
        P("width", None, None, None),
        P("width", None, None),
        P("width", None, None),
        P("dp", "width", None),
    )
    return jax.shard_map(
        shards,
        mesh=mesh,
        in_specs=placed,
        out_specs=(
            P("dp", "width", None),
            P("dp", "width", None),
            P("width", "dp", None, None),
            P("width", "dp", None),
            P("width", "dp", None),
        ),
        check_vma=False,
    )
```

time: 39 us -> 36.5 us (0.936)
  Pallas kernels: 38.2 us -> 35.7 us
    pallas_call x1, Pallas kernels: 37.2 us -> 34.8 us  [shards(): pl.pallas_call(functools.partial(step_kernel, n_dp, n_width, scale), out_...]
where the time goes in v1:
time: 36.5 us; the launch traced here: 36.4 us
  Pallas kernels  35.7 us (98%)
  between operations  0.64 us (2%)
    pallas_call x1, Pallas kernels, shards(): pl.pallas_call(functools.partial(step_kernel, n_dp, n_width, scale), out_...  34.8 us
    pallas_call x1, Pallas kernels, shards(): pl.pallas_call(hand_over, out_shape=tuple((jax.ShapeDtypeStruct(out.shape...  0.96 us

profile of v1, /device:TPU:0, one launch (start us, length us, event | category | flops | bytes accessed | tf_op | source)
XLA Modules:
  0.0 36.4 jit_solution(14786176468028506278)
XLA Ops:
  0.6 34.8 %shard_map.92 = (bf16[192,512]{1,0:T(8,128)(2,1)S(1)}, bf16[192,512]{1,0:T(8,128)(2,1)S(1)}, f32[3,64,512]{2,1,0:T(8,128)S(1)}, f32[64,256]{1,0:T(8,128)S(1)}, f32[32,512]{1,0:T(8,128)S(1)}) custom-call(bf16[192,512]{1,0:T(8,128)(2,1)} %bitcast.17, bf16[3,512,512]{2,1,0:T(8,128)(2,1)} %bitcast.14, bf16[512,256]{1,0:T(8,128)(2,1)} %bitcast.15, ...), custom_call_target="tpu_custom_call" | custom-call | tf_op jit(solution)/shard_map/pallas_call | solution.py:586
  35.4 1.0 %shard_map.93 = (bf16[192,512]{1,0:T(8,128)(2,1)}, bf16[192,512]{1,0:T(8,128)(2,1)}, f32[3,64,512]{2,1,0:T(8,128)}, f32[64,256]{1,0:T(8,128)}, f32[32,512]{1,0:T(8,128)}) custom-call(bf16[192,512]{1,0:T(8,128)(2,1)S(1)} %get-tuple-element.15.refs_0_, bf16[192,512]{1,0:T(8,128)(2,1)S(1)} %get-tuple-element.16.refs_1_, ...), custom_call_target="tpu_custom_call" | custom-call | tf_op jit(solution)/shard_map/pallas_call | solution.py:659

commit v2 on v1

--- a/solution.py
+++ b/solution.py
@@ -129,8 +129,7 @@
     away_r, own_r, core_r, far_r, near_r, end_r, fin_r,
     away_l, own_l, core_l, far_l, near_l, end_l, fin_l,
     load_sem, x_send, x_recv, lat_send, lat_recv, lg_send, lg_recv, back_send, back_recv,
-    up_send, up_recv, side_send, side_recv,
-    core_send, core_recv, mid_send, mid_recv, end_send, end_recv,
+    up_sem, side_send, side_recv, core_send, core_recv, mid_send, mid_recv, end_sem,
 ):
     levels = n_width.bit_length() - 1
     chips = n_dp // 2
@@ -201,20 +200,23 @@
     ends = jnp.where(chip == 0, 1, 0) + jnp.where(chip == chips - 1, 1, 0)
     pl.semaphore_wait(barrier, n_width + 2 - ends)
 
-    loads[0].wait()
     cut = rows // levels
+    lead = cut // 48 * 16
     parts = [pl.ds(j * cut, cut) for j in range(levels)]
     beyond = [pl.ds(rows + j * cut, cut) for j in range(levels)]
-    x_copies = [
-        [
+
+    def x_group(part, src, j):
+        return [
             remote(
-                x.at[0, part], x.at[bit + 1, part], x_send.at[j, bit], x_recv.at[j, bit],
-                dp, mate(1 << bit),
+                src.at[part], x.at[bit + 1, part], x_send, x_recv.at[j], dp, mate(1 << bit)
             )
             for bit in range(levels)
         ]
-        for j, part in enumerate(parts)
-    ]
+
+    x_lead = x_group(pl.ds(0, lead), x_hbm, 0)
+    x_copies = [x_group(pl.ds(lead, cut - lead), x.at[0], 0)]
+    for j in range(1, levels):
+        x_copies.append(x_group(parts[j], x.at[0], j))
 
     def exchange(sums, out, got, send, recv, t):
         copies = []
@@ -222,23 +224,29 @@
             out[t, part] = sums[part].astype(bf16)
             copies.append(
                 remote(
-                    out.at[t, part], got.at[t, part], send.at[t, j], recv.at[t, j],
+                    out.at[t, part], got.at[t, part], send, recv(t, j),
                     dp, mate(1 << (j + t) % levels),
                 )
             )
         for copy in copies:
             copy.start()
-        return copies
-
-    def merge(copies, sums, got, t, j):
-        copies[j].wait_recv()
-        sums[parts[j]] += got[t, parts[j]].astype(f32)
-
-    up_x = remote(x.at[0, mine], x.at[0, theirs], up_send.at[0], up_recv.at[0], hub_dp, me)
+
+    def arrived(ref, sem):
+        remote(ref, ref, core_send.at[0], sem, twin, me).wait_recv()
+
+    def left_here(ref, sem):
+        remote(ref, ref, sem, core_recv.at[0], twin, me).wait_send()
+
+    def lat_sem(t, j):
+        return lat_recv.at[t + (j if t == levels - 1 else 0)]
+
+    def lg_sem(t, j):
+        return lg_recv.at[t]
+
+    up_x = remote(x_hbm, x.at[0, theirs], up_sem.at[0], up_sem.at[0], hub_dp, me)
     side_copies = [
         remote(
-            x.at[0, theirs], x.at[bit + 1, theirs], side_send.at[bit], side_recv.at[bit],
-            dp, mate(1 << bit),
+            x.at[0, theirs], x.at[bit + 1, theirs], side_send, side_recv, dp, mate(1 << bit)
         )
         for bit in range(levels)
     ]
@@ -247,17 +255,20 @@
     def _():
         up_x.start()
 
+    for copy in x_lead:
+        copy.start()
+    loads[0].wait()
     loads[1].wait()
     lat_sum[...] = dot_nn(x[0, mine], left[...])
-    lat_copies = [exchange(lat_sum, lat_own, lat_got, lat_send, lat_recv, 0)]
+    exchange(lat_sum, lat_own, lat_got, lat_send, lat_sem, 0)
     for copy in x_copies[0]:
         copy.start()
     loads[2].wait()
     pre[...] = dot_nt(x[0, mine], w[0])
     for t in range(1, levels):
-        for j in range(levels):
-            merge(lat_copies[-1], lat_sum, lat_got, t - 1, j)
-        lat_copies.append(exchange(lat_sum, lat_own, lat_got, lat_send, lat_recv, t))
+        arrived(lat_got.at[t - 1], lat_recv.at[t - 1])
+        lat_sum[...] += lat_got[t - 1].astype(f32)
+        exchange(lat_sum, lat_own, lat_got, lat_send, lat_sem, t)
         for copy in x_copies[t]:
             copy.start()
     loads[3].wait()
@@ -273,27 +284,26 @@
         [
             remote(
                 hidden.at[part, span(p, 2 * ob)], hidden.at[away_part, span(p, 2 * ob)],
-                up_send.at[2 + levels + chips * j + p], up_recv.at[2 + levels + chips * j + p],
-                hub_dp, me,
+                up_sem.at[3 + min(p, 2)], up_sem.at[3 + min(p, 2)], hub_dp, me,
             )
             for p in range(chips)
         ]
-        for j, (part, away_part) in enumerate(zip(parts, beyond))
+        for part, away_part in zip(parts, beyond)
     ]
-    up_lat = [
-        remote(
-            lat.at[part], lat.at[away_part], up_send.at[2 + j], up_recv.at[2 + j], hub_dp, me
-        )
-        for j, (part, away_part) in enumerate(zip(parts, beyond))
+    up_lat = remote(lat.at[mine], lat.at[theirs], up_sem.at[1], up_sem.at[1], hub_dp, me)
+    up_lg = remote(lg.at[mine], lg.at[theirs], up_sem.at[2], up_sem.at[2], hub_dp, me)
+    up_views = [
+        x.at[0, theirs], lat.at[theirs], lg.at[theirs],
+        hidden.at[theirs, pl.ds(0, 2 * ob)], hidden.at[theirs, pl.ds(0, 2 * ob)],
+        hidden.at[theirs, pl.ds(0, 2 * ob * (chips - 2))],
     ]
-    up_lg = remote(lg.at[mine], lg.at[theirs], up_send.at[1], up_recv.at[1], hub_dp, me)
 
     for j, part in enumerate(parts):
-        merge(lat_copies[-1], lat_sum, lat_got, levels - 1, j)
-        lat[part, :] = lat_sum[part, :].astype(bf16)
+        arrived(lat_got.at[levels - 1, part], lat_sem(levels - 1, j))
+        lat[part, :] = (lat_sum[part, :] + lat_got[levels - 1, part].astype(f32)).astype(bf16)
         v = pre[part, :] + dot_nn(lat[part, :], right[...])
+        arrived(x.at[pl.ds(1, levels), part], x_recv.at[j])
         for bit in range(levels):
-            x_copies[j][bit].wait_recv()
             v = v + dot_nt(x[bit + 1, part], w[bit + 1])
         half = 0.5 * (1.0 + lax.erf(v * root_half))
         act_out[part, :] = (v * half).astype(bf16)
@@ -304,19 +314,20 @@
         def _():
             for p in range(2):
                 up_h[j][p].start()
-            up_lat[j].start()
+            if j == levels - 1:
+                up_lat.start()
 
         if j == 0:
 
             @pl.when(is_hub)
             def _():
-                up_x.wait_recv()
+                arrived(up_views[0], up_sem.at[0])
                 for copy in side_copies:
                     copy.start()
 
 
     lat_sum[...] = dot_nt(hidden[mine, :], right[...])
-    lg_copies = [exchange(lat_sum, lg_own, lg_got, lg_send, lg_recv, 0)]
+    exchange(lat_sum, lg_own, lg_got, lg_send, lg_sem, 0)
 
     def pick(kind, s):
         block, low_right, low_left = kind
@@ -333,21 +344,33 @@
     fin = (fin_b, fin_r, fin_l)
     segments = range(last + 2)
 
+    def kind_of(s):
+        return min(max(s - last + 1, 0), 2)
+
+    def core_slot(s, p):
+        if p > 1:
+            return levels + 4 + kind_of(s)
+        return p if s == 0 else s + 1
+
+    def mid_slot(s, p):
+        return s if p == 0 else levels + 3 + kind_of(s)
+
     def core_copy(s, p):
         return remote(
-            pick(away, s).at[p], pick(cored, s).at[p], core_send.at[s, p], core_recv.at[s, p],
-            twin, me,
+            pick(away, s).at[p], pick(cored, s).at[p],
+            core_send.at[kind_of(s)], core_recv.at[core_slot(s, p)], twin, me,
         )
 
     def mid_copy(s, p):
         return remote(
-            pick(far, s).at[p], pick(near, s).at[p], mid_send.at[s, p], mid_recv.at[s, p],
-            far_dp, me,
+            pick(far, s).at[p], pick(near, s).at[p],
+            mid_send.at[kind_of(s)], mid_recv.at[mid_slot(s, p)], far_dp, me,
         )
 
     def end_copy(s):
         return remote(
-            pick(ended, s), pick(fin, s), end_send.at[s], end_recv.at[s], end_dp, me
+            pick(ended, s), pick(fin, s), end_sem.at[kind_of(s)], end_sem.at[kind_of(s)],
+            end_dp, me,
         )
 
     def put(s, total):
@@ -360,19 +383,18 @@
 
     back_copies = [
         remote(
-            back_own.at[bit], back_got.at[bit], back_send.at[bit], back_recv.at[bit],
-            dp, mate(1 << bit),
+            back_own.at[bit], back_got.at[bit], back_send, back_recv, dp, mate(1 << bit)
         )
         for bit in range(levels)
     ]
 
     def lg_step(t):
-        for j in range(levels):
-            merge(lg_copies[-1], lat_sum, lg_got, t - 1, j)
+        arrived(lg_got.at[t - 1], lg_recv.at[t - 1])
         if t < levels:
-            lg_copies.append(exchange(lat_sum, lg_own, lg_got, lg_send, lg_recv, t))
+            lat_sum[...] += lg_got[t - 1].astype(f32)
+            exchange(lat_sum, lg_own, lg_got, lg_send, lg_sem, t)
         else:
-            lg[mine, :] = lat_sum[...].astype(bf16)
+            lg[mine, :] = (lat_sum[...] + lg_got[t - 1].astype(f32)).astype(bf16)
 
     def send_back():
         for bit in range(levels):
@@ -381,15 +403,16 @@
 
     def back_ready():
         total = dot_nn(hidden[mine, :], w[0]) + dot_nt(lg[mine, :], left[...])
+        arrived(back_got, back_recv)
         for bit in range(levels):
-            back_copies[bit].wait_recv()
             total = total + back_got[bit].astype(f32)
         in_out[...] = total.astype(bf16)
 
     def sent():
-        for group in x_copies + lat_copies + lg_copies + [back_copies]:
-            for copy in group:
-                copy.wait_send()
+        left_here(x.at[pl.ds(1, levels), mine], x_send)
+        left_here(lat_own, lat_send)
+        left_here(lg_own, lg_send)
+        left_here(back_own, back_send)
 
     @pl.when(is_end)
     def _():
@@ -403,17 +426,14 @@
         up_lg.start()
         back_ready()
         sent()
-        up_x.wait_send()
-        up_lg.wait_send()
-        for j in range(levels):
-            up_lat[j].wait_send()
-            for p in range(chips):
-                up_h[j][p].wait_send()
-        for s in segments:
-            end_copy(s).wait_recv()
+        for i, view in enumerate(up_views):
+            left_here(view, up_sem.at[i])
+        arrived(fin_b, end_sem.at[0])
+        for s in range(last):
+            put(s, fin_b[s].astype(f32))
+        for s in range(last, last + 2):
+            arrived(pick(fin, s), end_sem.at[kind_of(s)])
             put(s, pick(fin, s)[...].astype(f32))
-
-    del lg_copies[1:]
 
     @pl.when(is_hub)
     def _():
@@ -467,8 +487,15 @@
         def pair(s, p):
             return pick(own, s)[p] + pick(cored, s)[p].astype(f32)
 
+        def core_here(s, p):
+            both = pl.ds(0, 2)
+            if p > 1:
+                view = pick(cored, s).at[pl.ds(2, 2)] if s >= last else core_b.at[:, pl.ds(2, 2)]
+            else:
+                view = pick(cored, s).at[p if s == 0 else both]
+            arrived(view, core_recv.at[core_slot(s, p)])
+
         def send_far(s, p):
-            core_copy(s, p).wait_recv()
             pick(far, s)[p] = pair(s, p).astype(bf16)
             mid_copy(s, p).start()
 
@@ -479,28 +506,27 @@
             far_acc[s] = own_rows(s, other_core, range(2)).reshape(shape)
             own_b[s, 0:2] = own_rows(s, core, range(2)).reshape(shape)
         for p in range(2):
-            for j in range(levels):
-                up_h[j][p].wait_recv()
+            arrived(up_views[3 + p], up_sem.at[3 + p])
             h_u[p] = turn(hidden, theirs, p, 2 * ob)
             far_terms(0, [p])
         for p in range(2):
+            core_here(0, p)
             send_far(0, p)
+        arrived(x.at[pl.ds(1, levels), theirs], side_recv)
         for bit in range(levels):
-            side_copies[bit].wait_recv()
             far_terms(bit + 1, [0, 1])
         for t in range(1, levels):
             lg_step(t)
         send_back()
         for s in range(1, last):
-            for p in range(2):
-                send_far(s, p)
-        for j in range(levels):
-            up_lat[j].wait_recv()
+            core_here(s, 0)
+            send_far(s, 0)
+        for s in range(1, levels):
+            send_far(s, 1)
+        arrived(up_views[1], up_sem.at[1])
         lat_t[...] = lat[mine, :].astype(f32).T.astype(bf16).reshape(lat_t.shape)
         lat_u[...] = lat[theirs, :].astype(f32).T.astype(bf16).reshape(lat_t.shape)
-        for p in range(2, chips):
-            for j in range(levels):
-                up_h[j][p].wait_recv()
+        arrived(up_views[5], up_sem.at[5])
         terms(last, range(2))
         for p in range(2, chips):
             h_t[p] = turn(hidden, mine, p, 2 * ob)
@@ -508,46 +534,48 @@
         for s in range(last):
             terms(s, range(2, chips))
         terms(last, range(2, chips))
+        core_here(last, 0)
+        send_far(last, 0)
         for p in range(chips):
             x_t[p] = turn(x.at[0], mine, p, 2 * ib)
             x_u[p] = turn(x.at[0], theirs, p, 2 * ib)
         lg_step(levels)
-        up_lg.wait_recv()
+        arrived(up_views[2], up_sem.at[2])
         terms(last + 1, range(2))
-        for p in range(2):
-            send_far(last, p)
-            send_far(last + 1, p)
+        core_here(last + 1, 0)
+        send_far(last + 1, 0)
+        for s in range(levels, last + 2):
+            send_far(s, 1)
         terms(last + 1, range(2, chips))
 
         def send_end(s):
-            core_copy(s, 2).wait_recv()
-            mid_copy(s, 0).wait_recv()
+            arrived(pick(near, s).at[0], mid_recv.at[mid_slot(s, 0)])
             pick(ended, s)[...] = (pair(s, 2) + pick(near, s)[0].astype(f32)).astype(bf16)
             end_copy(s).start()
 
         def keep(s):
-            core_copy(s, 3).wait_recv()
-            mid_copy(s, 1).wait_recv()
             put(s, pair(s, 3) + pick(near, s)[1].astype(f32))
 
+        core_here(0, 2)
         for s in range(last):
             send_end(s)
-            keep(s)
         back_ready()
         sent()
-        for copy in side_copies:
-            copy.wait_send()
-        for s in segments:
-            for p in range(chips):
-                core_copy(s, p).wait_send()
-        send_end(last)
-        send_end(last + 1)
-        keep(last)
-        keep(last + 1)
-        for s in segments:
-            for p in range(2):
-                mid_copy(s, p).wait_send()
-            end_copy(s).wait_send()
+        left_here(x.at[pl.ds(1, levels), theirs], side_send)
+        for s in (0, last, last + 1):
+            left_here(away[kind_of(s)], core_send.at[kind_of(s)])
+        for s in (last, last + 1):
+            core_here(s, 2)
+            send_end(s)
+        arrived(near_b.at[:, 1], mid_recv.at[mid_slot(0, 1)])
+        for s in range(last):
+            keep(s)
+        for s in (last, last + 1):
+            arrived(pick(near, s).at[1], mid_recv.at[mid_slot(s, 1)])
+            keep(s)
+        for i in range(3):
+            left_here(far[i], mid_send.at[i])
+            left_here(ended[i], end_sem.at[i])
 
 
 def hand_over(*refs):
@@ -622,24 +650,22 @@
             *line_scratch((), rb, width_out),
             *line_scratch((), ib, rank),
             dma((5,)),
-            dma((levels, levels)),
-            dma((levels, levels)),
-            dma((levels, levels)),
-            dma((levels, levels)),
-            dma((levels, levels)),
-            dma((levels, levels)),
+            dma,
             dma((levels,)),
+            dma,
+            dma((2 * levels - 1,)),
+            dma,
             dma((levels,)),
-            dma((2 + levels * (1 + chips),)),
-            dma((2 + levels * (1 + chips),)),
-            dma((levels,)),
-            dma((levels,)),
-            dma((levels + 3, chips)),
-            dma((levels + 3, chips)),
-            dma((levels + 3, 2)),
-            dma((levels + 3, 2)),
-            dma((levels + 3,)),
-            dma((levels + 3,)),
+            dma,
+            dma,
+            dma((6,)),
+            dma,
+            dma,
+            dma((3,)),
+            dma((levels + 7,)),
+            dma((3,)),
+            dma((levels + 6,)),
+            dma((3,)),
         ],
         compiler_params=pltpu.CompilerParams(
             collective_id=0, has_side_effects=True, vmem_limit_bytes=40 * 1024 * 1024

time: 36.5 us -> 34.4 us (0.942)
  Pallas kernels: 35.7 us -> 33.6 us
    pallas_call x1, Pallas kernels: 34.8 us -> 32.6 us  [shards(): pl.pallas_call(functools.partial(step_kernel, n_dp, n_width, scale), out_...]
where the time goes in v2:
time: 34.4 us; the launch traced here: 34.2 us
  Pallas kernels  33.6 us (98%)
  between operations  0.64 us (2%)
    pallas_call x1, Pallas kernels, shards(): pl.pallas_call(functools.partial(step_kernel, n_dp, n_width, scale), out_...  32.6 us
    pallas_call x1, Pallas kernels, shards(): pl.pallas_call(hand_over, out_shape=tuple((jax.ShapeDtypeStruct(out.shape...  0.96 us

profile of v2, /device:TPU:0, one launch (start us, length us, event | category | flops | bytes accessed | tf_op | source)
XLA Modules:
  0.0 34.2 jit_solution(8076512649889839563)
XLA Ops:
  0.6 32.6 %shard_map.92 = (bf16[192,512]{1,0:T(8,128)(2,1)S(1)}, bf16[192,512]{1,0:T(8,128)(2,1)S(1)}, f32[3,64,512]{2,1,0:T(8,128)S(1)}, f32[64,256]{1,0:T(8,128)S(1)}, f32[32,512]{1,0:T(8,128)S(1)}) custom-call(bf16[192,512]{1,0:T(8,128)(2,1)} %bitcast.17, bf16[3,512,512]{2,1,0:T(8,128)(2,1)} %bitcast.14, bf16[512,256]{1,0:T(8,128)(2,1)} %bitcast.15, ...), custom_call_target="tpu_custom_call" | custom-call | tf_op jit(solution)/shard_map/pallas_call | solution.py:614
  33.3 1.0 %shard_map.93 = (bf16[192,512]{1,0:T(8,128)(2,1)}, bf16[192,512]{1,0:T(8,128)(2,1)}, f32[3,64,512]{2,1,0:T(8,128)}, f32[64,256]{1,0:T(8,128)}, f32[32,512]{1,0:T(8,128)}) custom-call(bf16[192,512]{1,0:T(8,128)(2,1)S(1)} %get-tuple-element.15.refs_0_, bf16[192,512]{1,0:T(8,128)(2,1)S(1)} %get-tuple-element.16.refs_1_, ...), custom_call_target="tpu_custom_call" | custom-call | tf_op jit(solution)/shard_map/pallas_call | solution.py:685

commit v3 on v2

--- a/solution.py
+++ b/solution.py
@@ -130,6 +130,7 @@
     away_l, own_l, core_l, far_l, near_l, end_l, fin_l,
     load_sem, x_send, x_recv, lat_send, lat_recv, lg_send, lg_recv, back_send, back_recv,
     up_sem, side_send, side_recv, core_send, core_recv, mid_send, mid_recv, end_sem,
+    pace,
 ):
     levels = n_width.bit_length() - 1
     chips = n_dp // 2
@@ -168,18 +169,6 @@
             device_id_type=pl.DeviceIdType.MESH,
         )
 
-    for k in range(1, n_width):
-        greet(dp, mate(k))
-    greet(twin, me)
-
-    @pl.when(chip > 0)
-    def _():
-        greet(dp - 2, me)
-
-    @pl.when(chip < chips - 1)
-    def _():
-        greet(dp + 2, me)
-
     rows = x_hbm.shape[0]
     mine, theirs = pl.ds(0, rows), pl.ds(rows, rows)
     loads = [
@@ -194,10 +183,26 @@
             )
         )
     ]
-    for load in loads:
+    for load in loads[:2]:
         load.start()
+    for k in range(1, n_width):
+        greet(dp, mate(k))
+    greet(twin, me)
+
+    @pl.when(chip > 0)
+    def _():
+        greet(dp - 2, me)
+
+    @pl.when(chip < chips - 1)
+    def _():
+        greet(dp + 2, me)
 
     ends = jnp.where(chip == 0, 1, 0) + jnp.where(chip == chips - 1, 1, 0)
+    loads[0].wait()
+    loads[1].wait()
+    for load in loads[2:]:
+        load.start()
+    lat_sum[...] = dot_nn(x[0, mine], left[...])
     pl.semaphore_wait(barrier, n_width + 2 - ends)
 
     cut = rows // levels
@@ -213,10 +218,7 @@
             for bit in range(levels)
         ]
 
-    x_lead = x_group(pl.ds(0, lead), x_hbm, 0)
-    x_copies = [x_group(pl.ds(lead, cut - lead), x.at[0], 0)]
-    for j in range(1, levels):
-        x_copies.append(x_group(parts[j], x.at[0], j))
+    x_copies = [x_group(part, x.at[0], j) for j, part in enumerate(parts)]
 
     def exchange(sums, out, got, send, recv, t):
         copies = []
@@ -237,6 +239,12 @@
     def left_here(ref, sem):
         remote(ref, ref, sem, core_recv.at[0], twin, me).wait_send()
 
+    def keep_pace():
+        pl.semaphore_signal(
+            pace, inc=1, device_id={"dp": twin, "width": me}, device_id_type=pl.DeviceIdType.MESH
+        )
+        pl.semaphore_wait(pace, 1)
+
     def lat_sem(t, j):
         return lat_recv.at[t + (j if t == levels - 1 else 0)]
 
@@ -255,12 +263,8 @@
     def _():
         up_x.start()
 
-    for copy in x_lead:
-        copy.start()
-    loads[0].wait()
-    loads[1].wait()
-    lat_sum[...] = dot_nn(x[0, mine], left[...])
     exchange(lat_sum, lat_own, lat_got, lat_send, lat_sem, 0)
+    keep_pace()
     for copy in x_copies[0]:
         copy.start()
     loads[2].wait()
@@ -298,13 +302,19 @@
         hidden.at[theirs, pl.ds(0, 2 * ob * (chips - 2))],
     ]
 
+    def add_mates(j):
+        arrived(x.at[pl.ds(1, levels), parts[j]], x_recv.at[j])
+        v = pre[parts[j], :]
+        for bit in range(levels):
+            v = v + dot_nt(x[bit + 1, parts[j]], w[bit + 1])
+        return v
+
+    pre[parts[0], :] = add_mates(0)
     for j, part in enumerate(parts):
         arrived(lat_got.at[levels - 1, part], lat_sem(levels - 1, j))
         lat[part, :] = (lat_sum[part, :] + lat_got[levels - 1, part].astype(f32)).astype(bf16)
-        v = pre[part, :] + dot_nn(lat[part, :], right[...])
-        arrived(x.at[pl.ds(1, levels), part], x_recv.at[j])
-        for bit in range(levels):
-            v = v + dot_nt(x[bit + 1, part], w[bit + 1])
+        pre[part, :] += dot_nn(lat[part, :], right[...])
+        v = add_mates(j) if j > 0 else pre[part, :]
         half = 0.5 * (1.0 + lax.erf(v * root_half))
         act_out[part, :] = (v * half).astype(bf16)
         slope = half + v * jnp.exp(-0.5 * v * v) * inv_root_two_pi
@@ -421,9 +431,9 @@
                 up_h[j][p].start()
         for t in range(1, levels + 1):
             lg_step(t)
-            if t == levels - 1:
-                send_back()
         up_lg.start()
+        keep_pace()
+        send_back()
         back_ready()
         sent()
         for i, view in enumerate(up_views):
@@ -509,9 +519,8 @@
             arrived(up_views[3 + p], up_sem.at[3 + p])
             h_u[p] = turn(hidden, theirs, p, 2 * ob)
             far_terms(0, [p])
-        for p in range(2):
-            core_here(0, p)
-            send_far(0, p)
+        core_here(0, 0)
+        send_far(0, 0)
         arrived(x.at[pl.ds(1, levels), theirs], side_recv)
         for bit in range(levels):
             far_terms(bit + 1, [0, 1])
@@ -521,8 +530,6 @@
         for s in range(1, last):
             core_here(s, 0)
             send_far(s, 0)
-        for s in range(1, levels):
-            send_far(s, 1)
         arrived(up_views[1], up_sem.at[1])
         lat_t[...] = lat[mine, :].astype(f32).T.astype(bf16).reshape(lat_t.shape)
         lat_u[...] = lat[theirs, :].astype(f32).T.astype(bf16).reshape(lat_t.shape)
@@ -536,17 +543,14 @@
         terms(last, range(2, chips))
         core_here(last, 0)
         send_far(last, 0)
+        core_here(0, 1)
+        send_far(0, 1)
         for p in range(chips):
             x_t[p] = turn(x.at[0], mine, p, 2 * ib)
             x_u[p] = turn(x.at[0], theirs, p, 2 * ib)
         lg_step(levels)
-        arrived(up_views[2], up_sem.at[2])
-        terms(last + 1, range(2))
-        core_here(last + 1, 0)
-        send_far(last + 1, 0)
-        for s in range(levels, last + 2):
-            send_far(s, 1)
-        terms(last + 1, range(2, chips))
+        own_first = own_rows(last + 1, other_core, range(chips))
+        own_second = own_rows(last + 1, core, range(chips))
 
         def send_end(s):
             arrived(pick(near, s).at[0], mid_recv.at[mid_slot(s, 0)])
@@ -557,7 +561,18 @@
             put(s, pair(s, 3) + pick(near, s)[1].astype(f32))
 
         core_here(0, 2)
-        for s in range(last):
+        send_end(0)
+        arrived(up_views[2], up_sem.at[2])
+        put_terms(
+            last + 1, range(chips), own_first + their_rows(last + 1, other_core, range(chips)),
+            own_second + their_rows(last + 1, core, range(chips)),
+        )
+        send_end(1)
+        core_here(last + 1, 0)
+        send_far(last + 1, 0)
+        for s in range(1, last + 2):
+            send_far(s, 1)
+        for s in range(2, last):
             send_end(s)
         back_ready()
         sent()
@@ -666,6 +681,7 @@
             dma((3,)),
             dma((levels + 6,)),
             dma((3,)),
+            pltpu.SemaphoreType.REGULAR,
         ],
         compiler_params=pltpu.CompilerParams(
             collective_id=0, has_side_effects=True, vmem_limit_bytes=40 * 1024 * 1024

time: 34.4 us -> 32.6 us (0.948)
  Pallas kernels: 33.6 us -> 31.8 us
    pallas_call x1, Pallas kernels: 32.6 us -> 30.8 us  [shards(): pl.pallas_call(functools.partial(step_kernel, n_dp, n_width, scale), out_...]
where the time goes in v3:
time: 32.6 us; the launch traced here: 32.4 us
  Pallas kernels  31.8 us (98%)
  between operations  0.64 us (2%)
    pallas_call x1, Pallas kernels, shards(): pl.pallas_call(functools.partial(step_kernel, n_dp, n_width, scale), out_...  30.8 us
    pallas_call x1, Pallas kernels, shards(): pl.pallas_call(hand_over, out_shape=tuple((jax.ShapeDtypeStruct(out.shape...  0.96 us

profile of v3, /device:TPU:0, one launch (start us, length us, event | category | flops | bytes accessed | tf_op | source)
XLA Modules:
  0.0 32.4 jit_solution(10401563459070404658)
XLA Ops:
  0.6 30.8 %shard_map.92 = (bf16[192,512]{1,0:T(8,128)(2,1)S(1)}, bf16[192,512]{1,0:T(8,128)(2,1)S(1)}, f32[3,64,512]{2,1,0:T(8,128)S(1)}, f32[64,256]{1,0:T(8,128)S(1)}, f32[32,512]{1,0:T(8,128)S(1)}) custom-call(bf16[192,512]{1,0:T(8,128)(2,1)} %bitcast.17, bf16[3,512,512]{2,1,0:T(8,128)(2,1)} %bitcast.14, bf16[512,256]{1,0:T(8,128)(2,1)} %bitcast.15, ...), custom_call_target="tpu_custom_call" | custom-call | tf_op jit(solution)/shard_map/pallas_call | solution.py:629
  31.5 1.0 %shard_map.93 = (bf16[192,512]{1,0:T(8,128)(2,1)}, bf16[192,512]{1,0:T(8,128)(2,1)}, f32[3,64,512]{2,1,0:T(8,128)}, f32[64,256]{1,0:T(8,128)}, f32[32,512]{1,0:T(8,128)}) custom-call(bf16[192,512]{1,0:T(8,128)(2,1)S(1)} %get-tuple-element.15.refs_0_, bf16[192,512]{1,0:T(8,128)(2,1)S(1)} %get-tuple-element.16.refs_1_, ...), custom_call_target="tpu_custom_call" | custom-call | tf_op jit(solution)/shard_map/pallas_call | solution.py:701

commit v4 on v3

--- a/solution.py
+++ b/solution.py
@@ -123,14 +123,14 @@
     act_out, in_out, block_out, left_out, right_out,
     x, w, left, right, g,
     lat_sum, lat_own, lat_got, lat, lg_own, lg_got, lg, hidden,
-    x_t, x_u, h_t, h_u, lat_t, lat_u, far_acc,
+    x_t, x_u, h_t, h_u, lat_t, lat_u, far_acc, x_far, h_far, h_v, h_w,
     back_own, back_got, pre,
     away_b, own_b, core_b, far_b, near_b, end_b, fin_b,
     away_r, own_r, core_r, far_r, near_r, end_r, fin_r,
     away_l, own_l, core_l, far_l, near_l, end_l, fin_l,
     load_sem, x_send, x_recv, lat_send, lat_recv, lg_send, lg_recv, back_send, back_recv,
     up_sem, side_send, side_recv, core_send, core_recv, mid_send, mid_recv, end_sem,
-    pace,
+    pace, over_send, over_recv,
 ):
     levels = n_width.bit_length() - 1
     chips = n_dp // 2
@@ -259,9 +259,20 @@
         for bit in range(levels)
     ]
 
+    over_x = [
+        remote(
+            x.at[0, these], x_far.at[these], over_send.at[0], over_recv.at[0], far_dp, me
+        )
+        for these in (mine, theirs)
+    ]
+
     @pl.when(is_end)
     def _():
         up_x.start()
+
+    @pl.when(is_hub)
+    def _():
+        over_x[0].start()
 
     exchange(lat_sum, lat_own, lat_got, lat_send, lat_sem, 0)
     keep_pace()
@@ -294,6 +305,12 @@
         ]
         for part, away_part in zip(parts, beyond)
     ]
+    def over_h(these, p):
+        return remote(
+            hidden.at[these, span(p, 2 * ob)], h_far.at[these, pl.ds(2 * ob * p, 2 * ob)],
+            over_send.at[1], over_recv.at[1], far_dp, me,
+        )
+
     up_lat = remote(lat.at[mine], lat.at[theirs], up_sem.at[1], up_sem.at[1], hub_dp, me)
     up_lg = remote(lg.at[mine], lg.at[theirs], up_sem.at[2], up_sem.at[2], hub_dp, me)
     up_views = [
@@ -327,17 +344,37 @@
             if j == levels - 1:
                 up_lat.start()
 
+        @pl.when(is_hub)
+        def _():
+            for p in range(2):
+                over_h(part, p).start()
+
         if j == 0:
 
             @pl.when(is_hub)
             def _():
                 arrived(up_views[0], up_sem.at[0])
+                over_x[1].start()
                 for copy in side_copies:
                     copy.start()
 
 
     lat_sum[...] = dot_nt(hidden[mine, :], right[...])
-    exchange(lat_sum, lg_own, lg_got, lg_send, lg_sem, 0)
+    spread = [
+        remote(lg_own.at[0], lg_got.at[k - 1], lg_send, lg_recv.at[0], dp, mate(k))
+        for k in reversed(range(1, n_width))
+    ]
+
+    @pl.when(is_hub)
+    def _():
+        exchange(lat_sum, lg_own, lg_got, lg_send, lg_sem, 0)
+
+    @pl.when(is_end)
+    def _():
+        lg_own[0] = lat_sum[...].astype(bf16)
+        for copy in spread:
+            copy.start()
+
 
     def pick(kind, s):
         block, low_right, low_left = kind
@@ -358,17 +395,15 @@
         return min(max(s - last + 1, 0), 2)
 
     def core_slot(s, p):
-        if p > 1:
-            return levels + 4 + kind_of(s)
-        return p if s == 0 else s + 1
+        return s - 1 if p < 2 else levels + 2 + kind_of(s)
 
     def mid_slot(s, p):
-        return s if p == 0 else levels + 3 + kind_of(s)
+        return s - 1 if p == 0 else levels + 2 + kind_of(s)
 
     def core_copy(s, p):
         return remote(
             pick(away, s).at[p], pick(cored, s).at[p],
-            core_send.at[kind_of(s)], core_recv.at[core_slot(s, p)], twin, me,
+            core_send.at[kind_of(s) if s else 3], core_recv.at[core_slot(s, p)], twin, me,
         )
 
     def mid_copy(s, p):
@@ -421,7 +456,6 @@
     def sent():
         left_here(x.at[pl.ds(1, levels), mine], x_send)
         left_here(lat_own, lat_send)
-        left_here(lg_own, lg_send)
         left_here(back_own, back_send)
 
     @pl.when(is_end)
@@ -429,13 +463,17 @@
         for j in range(levels):
             for p in range(2, chips):
                 up_h[j][p].start()
-        for t in range(1, levels + 1):
-            lg_step(t)
+        arrived(lg_got, lg_recv.at[0])
+        total = lat_sum[...]
+        for k in range(n_width - 1):
+            total = total + lg_got[k].astype(f32)
+        lg[mine, :] = total.astype(bf16)
         up_lg.start()
         keep_pace()
         send_back()
         back_ready()
         sent()
+        left_here(lg_got, lg_send)
         for i, view in enumerate(up_views):
             left_here(view, up_sem.at[i])
         arrived(fin_b, end_sem.at[0])
@@ -502,7 +540,7 @@
             if p > 1:
                 view = pick(cored, s).at[pl.ds(2, 2)] if s >= last else core_b.at[:, pl.ds(2, 2)]
             else:
-                view = pick(cored, s).at[p if s == 0 else both]
+                view = pick(cored, s).at[both]
             arrived(view, core_recv.at[core_slot(s, p)])
 
         def send_far(s, p):
@@ -511,16 +549,14 @@
 
         for p in range(2):
             h_t[p] = turn(hidden, mine, p, 2 * ob)
-        for s in range(last):
+        for s in range(1, last):
             shape = (2, ob, far_acc.shape[3])
             far_acc[s] = own_rows(s, other_core, range(2)).reshape(shape)
             own_b[s, 0:2] = own_rows(s, core, range(2)).reshape(shape)
         for p in range(2):
             arrived(up_views[3 + p], up_sem.at[3 + p])
+            over_h(theirs, p).start()
             h_u[p] = turn(hidden, theirs, p, 2 * ob)
-            far_terms(0, [p])
-        core_here(0, 0)
-        send_far(0, 0)
         arrived(x.at[pl.ds(1, levels), theirs], side_recv)
         for bit in range(levels):
             far_terms(bit + 1, [0, 1])
@@ -538,13 +574,25 @@
         for p in range(2, chips):
             h_t[p] = turn(hidden, mine, p, 2 * ob)
             h_u[p] = turn(hidden, theirs, p, 2 * ob)
-        for s in range(last):
+        for s in range(1, last):
             terms(s, range(2, chips))
         terms(last, range(2, chips))
         core_here(last, 0)
         send_far(last, 0)
-        core_here(0, 1)
-        send_far(0, 1)
+        send_far(1, 1)
+        arrived(x_far, over_recv.at[0])
+        arrived(h_far, over_recv.at[1])
+        for i in range(2):
+            cols = pl.ds(2 * ob * i, 2 * ob)
+            for these, ref in ((mine, h_v), (theirs, h_w)):
+                ref[i] = h_far[these, cols].astype(f32).T.astype(bf16).reshape(2, ob, rows)
+
+        def near_zero(which):
+            total = own_rows(0, which, range(2, chips)) + their_rows(0, which, range(2, chips))
+            total = total + dot_nn(stack(h_v, which, range(2)), x_far[mine, :])
+            return total + dot_nn(stack(h_w, which, range(2)), x_far[theirs, :])
+
+        put_terms(0, range(2, chips), near_zero(other_core), near_zero(core))
         for p in range(chips):
             x_t[p] = turn(x.at[0], mine, p, 2 * ib)
             x_u[p] = turn(x.at[0], theirs, p, 2 * ib)
@@ -553,12 +601,16 @@
         own_second = own_rows(last + 1, core, range(chips))
 
         def send_end(s):
-            arrived(pick(near, s).at[0], mid_recv.at[mid_slot(s, 0)])
-            pick(ended, s)[...] = (pair(s, 2) + pick(near, s)[0].astype(f32)).astype(bf16)
+            total = pair(s, 2)
+            if s > 0:
+                arrived(pick(near, s).at[0], mid_recv.at[mid_slot(s, 0)])
+                total = total + pick(near, s)[0].astype(f32)
+            pick(ended, s)[...] = total.astype(bf16)
             end_copy(s).start()
 
         def keep(s):
-            put(s, pair(s, 3) + pick(near, s)[1].astype(f32))
+            total = pair(s, 3)
+            put(s, total + pick(near, s)[1].astype(f32) if s > 0 else total)
 
         core_here(0, 2)
         send_end(0)
@@ -570,26 +622,32 @@
         send_end(1)
         core_here(last + 1, 0)
         send_far(last + 1, 0)
-        for s in range(1, last + 2):
+        for s in range(2, last + 2):
             send_far(s, 1)
         for s in range(2, last):
             send_end(s)
         back_ready()
         sent()
+        left_here(lg_own, lg_send)
         left_here(x.at[pl.ds(1, levels), theirs], side_send)
-        for s in (0, last, last + 1):
-            left_here(away[kind_of(s)], core_send.at[kind_of(s)])
+        left_here(away_b.at[0, pl.ds(2, 2)], core_send.at[3])
+        left_here(away_b.at[pl.ds(1, levels)], core_send.at[0])
+        left_here(away_r, core_send.at[1])
+        left_here(away_l, core_send.at[2])
+        left_here(x_far, over_send.at[0])
+        left_here(h_far, over_send.at[1])
         for s in (last, last + 1):
             core_here(s, 2)
             send_end(s)
-        arrived(near_b.at[:, 1], mid_recv.at[mid_slot(0, 1)])
-        for s in range(last):
+        keep(0)
+        arrived(near_b.at[pl.ds(1, levels), 1], mid_recv.at[mid_slot(1, 1)])
+        for s in range(1, last):
             keep(s)
         for s in (last, last + 1):
             arrived(pick(near, s).at[1], mid_recv.at[mid_slot(s, 1)])
             keep(s)
         for i in range(3):
-            left_here(far[i], mid_send.at[i])
+            left_here(far_b.at[pl.ds(1, levels)] if i == 0 else far[i], mid_send.at[i])
             left_here(ended[i], end_sem.at[i])
 
 
@@ -648,7 +706,7 @@
             vm((levels, rows, rank), bf16),
             vm((2 * rows, rank), bf16),
             vm((levels, rows, rank), bf16),
-            vm((levels, rows, rank), bf16),
+            vm((n_width - 1, rows, rank), bf16),
             vm((2 * rows, rank), bf16),
             vm((2 * rows, width_out), bf16),
             vm((chips, 2, ib, rows), bf16),
@@ -658,6 +716,10 @@
             vm((chips, 2, rb, rows), bf16),
             vm((chips, 2, rb, rows), bf16),
             vm((levels + 1, 2, ob, width_in), f32),
+            vm((2 * rows, width_in), bf16),
+            vm((2 * rows, 4 * ob), bf16),
+            vm((2, 2, ob, rows), bf16),
+            vm((2, 2, ob, rows), bf16),
             vm((levels, rows, width_in), bf16),
             vm((levels, rows, width_in), bf16),
             vm((rows, width_out), f32),
@@ -676,12 +738,14 @@
             dma((6,)),
             dma,
             dma,
+            dma((4,)),
+            dma((levels + 5,)),
             dma((3,)),
-            dma((levels + 7,)),
-            dma((3,)),
-            dma((levels + 6,)),
+            dma((levels + 5,)),
             dma((3,)),
             pltpu.SemaphoreType.REGULAR,
+            dma((2,)),
+            dma((2,)),
         ],
         compiler_params=pltpu.CompilerParams(
             collective_id=0, has_side_effects=True, vmem_limit_bytes=40 * 1024 * 1024

time: 32.6 us -> 32.4 us (level)
  no operation moved by 1% of the time
where the time goes in v4:
time: 32.4 us; the launch traced here: 32.2 us
  Pallas kernels  31.5 us (97%)
  between operations  0.64 us (2%)
    pallas_call x1, Pallas kernels, shards(): pl.pallas_call(functools.partial(step_kernel, n_dp, n_width, scale), out_...  30.6 us
    pallas_call x1, Pallas kernels, shards(): pl.pallas_call(hand_over, out_shape=tuple((jax.ShapeDtypeStruct(out.shape...  0.96 us

profile of v4, /device:TPU:0, one launch (start us, length us, event | category | flops | bytes accessed | tf_op | source)
XLA Modules:
  0.0 32.2 jit_solution(9951130589398544551)
XLA Ops:
  0.6 30.6 %shard_map.92 = (bf16[192,512]{1,0:T(8,128)(2,1)S(1)}, bf16[192,512]{1,0:T(8,128)(2,1)S(1)}, f32[3,64,512]{2,1,0:T(8,128)S(1)}, f32[64,256]{1,0:T(8,128)S(1)}, f32[32,512]{1,0:T(8,128)S(1)}) custom-call(bf16[192,512]{1,0:T(8,128)(2,1)} %bitcast.17, bf16[3,512,512]{2,1,0:T(8,128)(2,1)} %bitcast.14, bf16[512,256]{1,0:T(8,128)(2,1)} %bitcast.15, ...), custom_call_target="tpu_custom_call" | custom-call | tf_op jit(solution)/shard_map/pallas_call | solution.py:687
  31.2 1.0 %shard_map.93 = (bf16[192,512]{1,0:T(8,128)(2,1)}, bf16[192,512]{1,0:T(8,128)(2,1)}, f32[3,64,512]{2,1,0:T(8,128)}, f32[64,256]{1,0:T(8,128)}, f32[32,512]{1,0:T(8,128)}) custom-call(bf16[192,512]{1,0:T(8,128)(2,1)S(1)} %get-tuple-element.15.refs_0_, bf16[192,512]{1,0:T(8,128)(2,1)S(1)} %get-tuple-element.16.refs_1_, ...), custom_call_target="tpu_custom_call" | custom-call | tf_op jit(solution)/shard_map/pallas_call | solution.py:765

commit v5 on v4

--- a/solution.py
+++ b/solution.py
@@ -251,7 +251,11 @@
     def lg_sem(t, j):
         return lg_recv.at[t]
 
-    up_x = remote(x_hbm, x.at[0, theirs], up_sem.at[0], up_sem.at[0], hub_dp, me)
+    later, later_there = pl.ds(cut, rows - cut), pl.ds(rows + cut, rows - cut)
+    up_x = [
+        remote(x_hbm.at[part], x.at[0, there], up_sem.at[i], up_sem.at[i], hub_dp, me)
+        for i, part, there in ((0, parts[0], beyond[0]), (6, later, later_there))
+    ]
     side_copies = [
         remote(
             x.at[0, theirs], x.at[bit + 1, theirs], side_send, side_recv, dp, mate(1 << bit)
@@ -263,12 +267,13 @@
         remote(
             x.at[0, these], x_far.at[these], over_send.at[0], over_recv.at[0], far_dp, me
         )
-        for these in (mine, theirs)
+        for these in (mine, beyond[0], later_there)
     ]
 
     @pl.when(is_end)
     def _():
-        up_x.start()
+        for copy in up_x:
+            copy.start()
 
     @pl.when(is_hub)
     def _():
@@ -311,12 +316,15 @@
             over_send.at[1], over_recv.at[1], far_dp, me,
         )
 
-    up_lat = remote(lat.at[mine], lat.at[theirs], up_sem.at[1], up_sem.at[1], hub_dp, me)
+    up_lat = [
+        remote(lat.at[part], lat.at[away_part], up_sem.at[1], up_sem.at[1], hub_dp, me)
+        for part, away_part in zip(parts, beyond)
+    ]
     up_lg = remote(lg.at[mine], lg.at[theirs], up_sem.at[2], up_sem.at[2], hub_dp, me)
     up_views = [
-        x.at[0, theirs], lat.at[theirs], lg.at[theirs],
+        x.at[0, beyond[0]], lat.at[theirs], lg.at[theirs],
         hidden.at[theirs, pl.ds(0, 2 * ob)], hidden.at[theirs, pl.ds(0, 2 * ob)],
-        hidden.at[theirs, pl.ds(0, 2 * ob * (chips - 2))],
+        hidden.at[theirs, pl.ds(0, 2 * ob * (chips - 2))], x.at[0, later_there],
     ]
 
     def add_mates(j):
@@ -327,9 +335,20 @@
         return v
 
     pre[parts[0], :] = add_mates(0)
+
+    @pl.when(is_hub)
+    def _():
+        arrived(up_views[0], up_sem.at[0])
+        over_x[1].start()
+
     for j, part in enumerate(parts):
         arrived(lat_got.at[levels - 1, part], lat_sem(levels - 1, j))
         lat[part, :] = (lat_sum[part, :] + lat_got[levels - 1, part].astype(f32)).astype(bf16)
+
+        @pl.when(is_end)
+        def _():
+            up_lat[j].start()
+
         pre[part, :] += dot_nn(lat[part, :], right[...])
         v = add_mates(j) if j > 0 else pre[part, :]
         half = 0.5 * (1.0 + lax.erf(v * root_half))
@@ -341,8 +360,6 @@
         def _():
             for p in range(2):
                 up_h[j][p].start()
-            if j == levels - 1:
-                up_lat.start()
 
         @pl.when(is_hub)
         def _():
@@ -353,27 +370,31 @@
 
             @pl.when(is_hub)
             def _():
-                arrived(up_views[0], up_sem.at[0])
-                over_x[1].start()
+                arrived(up_views[6], up_sem.at[6])
+                over_x[2].start()
                 for copy in side_copies:
                     copy.start()
 
 
     lat_sum[...] = dot_nt(hidden[mine, :], right[...])
-    spread = [
-        remote(lg_own.at[0], lg_got.at[k - 1], lg_send, lg_recv.at[0], dp, mate(k))
-        for k in reversed(range(1, n_width))
-    ]
-
-    @pl.when(is_hub)
+    gathers = outer + core == 0
+
+    @pl.when(outer + core > 0)
     def _():
         exchange(lat_sum, lg_own, lg_got, lg_send, lg_sem, 0)
 
-    @pl.when(is_end)
+    @pl.when(gathers)
     def _():
         lg_own[0] = lat_sum[...].astype(bf16)
-        for copy in spread:
-            copy.start()
+        for at in range(n_width):
+
+            @pl.when(me == at)
+            def _():
+                order = [k for k in (at, *reversed(range(1, n_width))) if k > 0]
+                for k in dict.fromkeys(order):
+                    remote(
+                        lg_own.at[0], lg_got.at[k - 1], lg_send, lg_recv.at[0], dp, mate(k)
+                    ).start()
 
 
     def pick(kind, s):
@@ -460,20 +481,41 @@
 
     @pl.when(is_end)
     def _():
-        for j in range(levels):
-            for p in range(2, chips):
-                up_h[j][p].start()
-        arrived(lg_got, lg_recv.at[0])
-        total = lat_sum[...]
-        for k in range(n_width - 1):
-            total = total + lg_got[k].astype(f32)
-        lg[mine, :] = total.astype(bf16)
+        def send_near():
+            for j in range(levels):
+                for p in range(2, chips):
+                    up_h[j][p].start()
+
+        @pl.when(gathers)
+        def _():
+            send_near()
+            arrived(lg_got, lg_recv.at[0])
+            total = lat_sum[...]
+            for k in range(n_width - 1):
+                total = total + lg_got[k].astype(f32)
+            lg[mine, :] = total.astype(bf16)
+
+        @pl.when(outer + core > 0)
+        def _():
+            for t in range(1, levels + 1):
+                lg_step(t)
+                if t == 1:
+                    send_near()
+
         up_lg.start()
         keep_pace()
         send_back()
         back_ready()
         sent()
-        left_here(lg_got, lg_send)
+
+        @pl.when(gathers)
+        def _():
+            left_here(lg_got, lg_send)
+
+        @pl.when(outer + core > 0)
+        def _():
+            left_here(lg_own, lg_send)
+
         for i, view in enumerate(up_views):
             left_here(view, up_sem.at[i])
         arrived(fin_b, end_sem.at[0])
@@ -615,10 +657,15 @@
         core_here(0, 2)
         send_end(0)
         arrived(up_views[2], up_sem.at[2])
-        put_terms(
-            last + 1, range(chips), own_first + their_rows(last + 1, other_core, range(chips)),
-            own_second + their_rows(last + 1, core, range(chips)),
-        )
+        for part in (range(2), range(2, chips)):
+            held = slice(part[0] * ib, (part[-1] + 1) * ib)
+            to_other = own_first[held] + their_rows(last + 1, other_core, part)
+            for i, p in enumerate(part):
+                away_l[p] = to_other[i * ib : (i + 1) * ib].astype(bf16)
+                core_copy(last + 1, p).start()
+        to_own = own_second + their_rows(last + 1, core, range(chips))
+        for p in range(chips):
+            own_l[p] = to_own[p * ib : (p + 1) * ib]
         send_end(1)
         core_here(last + 1, 0)
         send_far(last + 1, 0)
@@ -667,7 +714,7 @@
     rank = low_left.shape[2]
     ob, ib, rb = width_out // n_dp, width_in // n_dp, rank // n_dp
     fits = n_dp == 2 * chips_in_line and rows % (16 * n_width) == 0 and rows % 32 == 0 and width_in == width_out
-    if not fits or ob % 64 or ib % 64 or rb % 16 or levels < 1 or rows % (16 * levels) or rank % 128:
+    if not fits or ob % 64 or ib % 64 or rb % 16 or levels < 2 or rows % (16 * levels) or rank % 128:
         return plain_shards(inputs, block_weights, low_left, low_right, out_grad)
     chips = n_dp // 2
     scale = 1.0 / math.sqrt(rows * n_dp)
@@ -735,7 +782,7 @@
             dma((levels,)),
             dma,
             dma,
-            dma((6,)),
+            dma((7,)),
             dma,
             dma,
             dma((4,)),

time: 32.4 us -> 32.1 us (level)
  no operation moved by 1% of the time
where the time goes in v5:
time: 32.1 us; the launch traced here: 31.9 us
  Pallas kernels  31.3 us (98%)
  between operations  0.64 us (2%)
    pallas_call x1, Pallas kernels, shards(): pl.pallas_call(functools.partial(step_kernel, n_dp, n_width, scale), out_...  30.3 us
    pallas_call x1, Pallas kernels, shards(): pl.pallas_call(hand_over, out_shape=tuple((jax.ShapeDtypeStruct(out.shape...  0.96 us

profile of v5, /device:TPU:0, one launch (start us, length us, event | category | flops | bytes accessed | tf_op | source)
XLA Modules:
  0.0 31.9 jit_solution(286963296246925296)
XLA Ops:
  0.6 30.3 %shard_map.92 = (bf16[192,512]{1,0:T(8,128)(2,1)S(1)}, bf16[192,512]{1,0:T(8,128)(2,1)S(1)}, f32[3,64,512]{2,1,0:T(8,128)S(1)}, f32[64,256]{1,0:T(8,128)S(1)}, f32[32,512]{1,0:T(8,128)S(1)}) custom-call(bf16[192,512]{1,0:T(8,128)(2,1)} %bitcast.17, bf16[3,512,512]{2,1,0:T(8,128)(2,1)} %bitcast.14, bf16[512,256]{1,0:T(8,128)(2,1)} %bitcast.15, ...), custom_call_target="tpu_custom_call" | custom-call | tf_op jit(solution)/shard_map/pallas_call | solution.py:734
  31.0 1.0 %shard_map.93 = (bf16[192,512]{1,0:T(8,128)(2,1)}, bf16[192,512]{1,0:T(8,128)(2,1)}, f32[3,64,512]{2,1,0:T(8,128)}, f32[64,256]{1,0:T(8,128)}, f32[32,512]{1,0:T(8,128)}) custom-call(bf16[192,512]{1,0:T(8,128)(2,1)S(1)} %get-tuple-element.15.refs_0_, bf16[192,512]{1,0:T(8,128)(2,1)S(1)} %get-tuple-element.16.refs_1_, ...), custom_call_target="tpu_custom_call" | custom-call | tf_op jit(solution)/shard_map/pallas_call | solution.py:812

commit v6 on v5

--- a/solution.py
+++ b/solution.py
@@ -327,6 +327,22 @@
         hidden.at[theirs, pl.ds(0, 2 * ob * (chips - 2))], x.at[0, later_there],
     ]
 
+    gathers = outer + core == 0
+
+    def gather_part(part):
+        lat_sum[part, :] = dot_nt(hidden[part, :], right[...])
+        lg_own[0, part] = lat_sum[part, :].astype(bf16)
+        for at in range(n_width):
+
+            @pl.when(me == at)
+            def _():
+                order = [k for k in (at, *reversed(range(1, n_width))) if k > 0]
+                for k in dict.fromkeys(order):
+                    remote(
+                        lg_own.at[0, part], lg_got.at[k - 1, part], lg_send, lg_recv.at[0],
+                        dp, mate(k),
+                    ).start()
+
     def add_mates(j):
         arrived(x.at[pl.ds(1, levels), parts[j]], x_recv.at[j])
         v = pre[parts[j], :]
@@ -361,6 +377,10 @@
             for p in range(2):
                 up_h[j][p].start()
 
+        @pl.when(gathers)
+        def _():
+            gather_part(part)
+
         @pl.when(is_hub)
         def _():
             for p in range(2):
@@ -376,25 +396,10 @@
                     copy.start()
 
 
-    lat_sum[...] = dot_nt(hidden[mine, :], right[...])
-    gathers = outer + core == 0
-
     @pl.when(outer + core > 0)
     def _():
+        lat_sum[...] = dot_nt(hidden[mine, :], right[...])
         exchange(lat_sum, lg_own, lg_got, lg_send, lg_sem, 0)
-
-    @pl.when(gathers)
-    def _():
-        lg_own[0] = lat_sum[...].astype(bf16)
-        for at in range(n_width):
-
-            @pl.when(me == at)
-            def _():
-                order = [k for k in (at, *reversed(range(1, n_width))) if k > 0]
-                for k in dict.fromkeys(order):
-                    remote(
-                        lg_own.at[0], lg_got.at[k - 1], lg_send, lg_recv.at[0], dp, mate(k)
-                    ).start()
 
 
     def pick(kind, s):
@@ -621,7 +626,6 @@
         terms(last, range(2, chips))
         core_here(last, 0)
         send_far(last, 0)
-        send_far(1, 1)
         arrived(x_far, over_recv.at[0])
         arrived(h_far, over_recv.at[1])
         for i in range(2):
@@ -669,10 +673,12 @@
         send_end(1)
         core_here(last + 1, 0)
         send_far(last + 1, 0)
-        for s in range(2, last + 2):
+        for s in range(1, last + 2):
             send_far(s, 1)
         for s in range(2, last):
             send_end(s)
+        core_here(last, 2)
+        send_end(last)
         back_ready()
         sent()
         left_here(lg_own, lg_send)
@@ -683,9 +689,8 @@
         left_here(away_l, core_send.at[2])
         left_here(x_far, over_send.at[0])
         left_here(h_far, over_send.at[1])
-        for s in (last, last + 1):
-            core_here(s, 2)
-            send_end(s)
+        core_here(last + 1, 2)
+        send_end(last + 1)
         keep(0)
         arrived(near_b.at[pl.ds(1, levels), 1], mid_recv.at[mid_slot(1, 1)])
         for s in range(1, last):

time: 32.1 us -> 31.9 us (level)
  no operation moved by 1% of the time
where the time goes in v6:
time: 31.9 us; the launch traced here: 31.7 us
  Pallas kernels  31.1 us (97%)
  between operations  0.64 us (2%)
    pallas_call x1, Pallas kernels, shards(): pl.pallas_call(functools.partial(step_kernel, n_dp, n_width, scale), out_...  30.1 us
    pallas_call x1, Pallas kernels, shards(): pl.pallas_call(hand_over, out_shape=tuple((jax.ShapeDtypeStruct(out.shape...  0.96 us

profile of v6, /device:TPU:0, one launch (start us, length us, event | category | flops | bytes accessed | tf_op | source)
XLA Modules:
  0.0 31.7 jit_solution(7440161826741911050)
XLA Ops:
  0.6 30.1 %shard_map.92 = (bf16[192,512]{1,0:T(8,128)(2,1)S(1)}, bf16[192,512]{1,0:T(8,128)(2,1)S(1)}, f32[3,64,512]{2,1,0:T(8,128)S(1)}, f32[64,256]{1,0:T(8,128)S(1)}, f32[32,512]{1,0:T(8,128)S(1)}) custom-call(bf16[192,512]{1,0:T(8,128)(2,1)} %bitcast.17, bf16[3,512,512]{2,1,0:T(8,128)(2,1)} %bitcast.14, bf16[512,256]{1,0:T(8,128)(2,1)} %bitcast.15, ...), custom_call_target="tpu_custom_call" | custom-call | tf_op jit(solution)/shard_map/pallas_call | solution.py:739
  30.7 1.0 %shard_map.93 = (bf16[192,512]{1,0:T(8,128)(2,1)}, bf16[192,512]{1,0:T(8,128)(2,1)}, f32[3,64,512]{2,1,0:T(8,128)}, f32[64,256]{1,0:T(8,128)}, f32[32,512]{1,0:T(8,128)}) custom-call(bf16[192,512]{1,0:T(8,128)(2,1)S(1)} %get-tuple-element.15.refs_0_, bf16[192,512]{1,0:T(8,128)(2,1)S(1)} %get-tuple-element.16.refs_1_, ...), custom_call_target="tpu_custom_call" | custom-call | tf_op jit(solution)/shard_map/pallas_call | solution.py:817

commit v7 on v6

--- a/solution.py
+++ b/solution.py
@@ -661,18 +661,25 @@
         core_here(0, 2)
         send_end(0)
         arrived(up_views[2], up_sem.at[2])
-        for part in (range(2), range(2, chips)):
+        def left_terms(part):
             held = slice(part[0] * ib, (part[-1] + 1) * ib)
             to_other = own_first[held] + their_rows(last + 1, other_core, part)
             for i, p in enumerate(part):
                 away_l[p] = to_other[i * ib : (i + 1) * ib].astype(bf16)
                 core_copy(last + 1, p).start()
-        to_own = own_second + their_rows(last + 1, core, range(chips))
-        for p in range(chips):
-            own_l[p] = to_own[p * ib : (p + 1) * ib]
+            to_own = own_second[held] + their_rows(last + 1, core, part)
+            for i, p in enumerate(part):
+                own_l[p] = to_own[i * ib : (i + 1) * ib]
+
+        def send_left():
+            core_here(last + 1, 0)
+            send_far(last + 1, 0)
+
+        left_terms(range(2))
+        pl.when(side + other_core == 2)(send_left)
+        left_terms(range(2, chips))
         send_end(1)
-        core_here(last + 1, 0)
-        send_far(last + 1, 0)
+        pl.when(side + other_core < 2)(send_left)
         for s in range(1, last + 2):
             send_far(s, 1)
         for s in range(2, last):

time: 31.9 us -> 31.9 us (level)
  no operation moved by 1% of the time
where the time goes in v7:
time: 31.9 us; the launch traced here: 31.7 us
  Pallas kernels  31.1 us (97%)
  between operations  0.64 us (2%)
    pallas_call x1, Pallas kernels, shards(): pl.pallas_call(functools.partial(step_kernel, n_dp, n_width, scale), out_...  30.1 us
    pallas_call x1, Pallas kernels, shards(): pl.pallas_call(hand_over, out_shape=tuple((jax.ShapeDtypeStruct(out.shape...  0.96 us

profile of v7, /device:TPU:0, one launch (start us, length us, event | category | flops | bytes accessed | tf_op | source)
XLA Modules:
  0.0 31.7 jit_solution(3395615182794969269)
XLA Ops:
  0.6 30.1 %shard_map.92 = (bf16[192,512]{1,0:T(8,128)(2,1)S(1)}, bf16[192,512]{1,0:T(8,128)(2,1)S(1)}, f32[3,64,512]{2,1,0:T(8,128)S(1)}, f32[64,256]{1,0:T(8,128)S(1)}, f32[32,512]{1,0:T(8,128)S(1)}) custom-call(bf16[192,512]{1,0:T(8,128)(2,1)} %bitcast.17, bf16[3,512,512]{2,1,0:T(8,128)(2,1)} %bitcast.14, bf16[512,256]{1,0:T(8,128)(2,1)} %bitcast.15, ...), custom_call_target="tpu_custom_call" | custom-call | tf_op jit(solution)/shard_map/pallas_call | solution.py:746
  30.7 1.0 %shard_map.93 = (bf16[192,512]{1,0:T(8,128)(2,1)}, bf16[192,512]{1,0:T(8,128)(2,1)}, f32[3,64,512]{2,1,0:T(8,128)}, f32[64,256]{1,0:T(8,128)}, f32[32,512]{1,0:T(8,128)}) custom-call(bf16[192,512]{1,0:T(8,128)(2,1)S(1)} %get-tuple-element.15.refs_0_, bf16[192,512]{1,0:T(8,128)(2,1)S(1)} %get-tuple-element.16.refs_1_, ...), custom_call_target="tpu_custom_call" | custom-call | tf_op jit(solution)/shard_map/pallas_call | solution.py:824
